TPU v7x, 32 devices: a whole 2x2x4 slice. The times are simulated.
32 devices in a mesh: hor: 4 (over y, core), lat: 8 (over z, x).
Axes of the slice: x: 2, y: 2, z: 4, core: 2. Of those that a mesh axis runs over, the one named last changes fastest.
Arguments:
- window: float32 [4, 69, 64, 128], P('hor', None, 'lat'), may hold values from -6 to 6
- fresh_noise: float32 [69, 64, 128], P(None, 'lat'), may hold values from -6 to 6
- level_index: int32 [4], P('hor'), may hold values from 4 to 63
- plan: float32 [64], replicated, may hold values from 0.07 to 38.42, as said below
- retention: float32 [4, 192], P('hor'), may hold values from 0.12 to 1
- lift_weight: bfloat16 [192, 69], replicated, may hold values from -0.75 to 0.75
- mod_scale: float32 [192], replicated, may hold values from -3 to 3
- mod_shift: float32 [192], replicated, may hold values from -3 to 3
- conv_weight: bfloat16 [3, 192, 576], replicated, may hold values from -0.15625 to 0.15625
- out_weight: bfloat16 [69, 192], replicated, may hold values from -0.4375 to 0.4375
Outputs:
- window_out: float32 [4, 69, 64, 128], P('hor', None, 'lat')
- rolled: float32 [4, 69, 64, 128], P('hor', None, 'lat')
Inputs may be any that keep to these rules, and one draw needn't show every extreme that they name: `plan`: rising from each entry to the next.
All inputs are finite; a program needn't handle non-finite values.
Results may differ from a plain program's by a relative error of at most 0.00064.
Values may be sent and summed in bfloat16 or wider, within the bound.
A program may use at most 64 MiB of HBM per device.

v0:
```python
import functools

import jax
import jax.numpy as jnp
from jax import lax
from jax.experimental import pallas as pl
from jax.experimental.pallas import tpu as pltpu
from jax.sharding import PartitionSpec as P

POOL = 4
STEPS = 3
MESH = pl.DeviceIdType.MESH
F32 = jnp.float32
BF16 = jnp.bfloat16
WIRE = jnp.bfloat16


def dot(a, b):
    return jnp.dot(a, b, preferred_element_type=F32)


def silu(x):
    h = 0.5 * x
    return h + h * jnp.tanh(h)


def kernel(
    rows,
    lon,
    n_hor,
    n_lat,
    lvl,
    plan,
    win_h,
    fresh_h,
    ret_h,
    msc_h,
    msh_h,
    lift_h,
    convw_h,
    outw_h,
    wout,
    arr,
    win,
    ret,
    msc,
    msh,
    liftt,
    convw,
    outw,
    liftw,
    base_send,
    base_recv,
    gain_send,
    gain_recv,
    cur,
    stack,
    acc,
    up,
    coef,
    mods,
    poolm,
    spread,
    ctx,
    hsend,
    hrecv,
    psend,
    precv,
    rrecv,
    h_ssem,
    h_rsem,
    p_ssem,
    p_rsem,
    r_ssem,
    r_rsem,
    l_sem,
    f_sem,
    g_ssem,
    g_rsem,
):
    hidden, chans = liftw.shape
    half = hidden // 2
    pair = 2 * lon
    n_pairs = rows // 2
    hor = lax.axis_index("hor")
    lat = lax.axis_index("lat")

    barrier = pltpu.get_barrier_semaphore()

    @pl.when(lat > 0)
    def _():
        pl.semaphore_signal(barrier, inc=1, device_id={"lat": lat - 1}, device_id_type=MESH)

    @pl.when(lat < n_lat - 1)
    def _():
        pl.semaphore_signal(barrier, inc=1, device_id={"lat": lat + 1}, device_id_type=MESH)

    for d in range(1, n_hor):
        pl.semaphore_signal(
            barrier, inc=1, device_id={"hor": lax.rem(hor + d, n_hor)}, device_id_type=MESH
        )

    pairs = [(win_h, win), (msc_h, msc), (msh_h, msh), (ret_h, ret), (lift_h, liftt)]
    pairs += [(convw_h, convw), (outw_h, outw)]
    loads = [pltpu.make_async_copy(a, b, l_sem.at[i]) for i, (a, b) in enumerate(pairs)]
    fresh_load = pltpu.make_async_copy(fresh_h, arr, l_sem.at[len(pairs)])
    for load in loads:
        load.start()

    @pl.when(hor == n_hor - 1)
    def _():
        fresh_load.start()

    for side in range(2):

        @pl.when(jnp.logical_not(lat > 0 if side == 0 else lat < n_lat - 1))
        def _():
            hrecv[:, side] = jnp.zeros_like(hrecv[:, side])

    def column(row_ref_value, start, count):
        sub = lax.broadcasted_iota(jnp.int32, (count, hidden), 0) + start
        lane = lax.broadcasted_iota(jnp.int32, (count, hidden), 1)
        return jnp.sum(jnp.where(sub == lane, row_ref_value, 0.0), axis=1, keepdims=True)

    def packed_rate(value):
        lane = lax.broadcasted_iota(jnp.int32, (half, lon), 1)
        lo = jnp.broadcast_to(column(value, 0, half), (half, lon))
        hi = jnp.broadcast_to(column(value, half, half), (half, lon))
        return jnp.where(lane < lon // 2, lo, hi)

    groups = lon // POOL
    for tok in range(rows // POOL):
        for side in range(2):
            k = lax.broadcasted_iota(jnp.int32, (pair, lon), 0)
            n = lax.broadcasted_iota(jnp.int32, (pair, lon), 1)
            want = side * (lon // 2) + tok * groups + lax.shift_right_logical(
                lax.bitwise_and(k, lon - 1), POOL.bit_length() - 1
            )
            poolm[2 * tok + side] = jnp.where(want == n, 1.0 / (POOL * POOL), 0.0).astype(BF16)
    for side in range(2):
        k = lax.broadcasted_iota(jnp.int32, (2 * lon, pair), 0)
        n = lax.broadcasted_iota(jnp.int32, (2 * lon, pair), 1)
        want = side * (lon // 2) + lax.shift_right_logical(n, POOL.bit_length() - 1)
        spread[side] = jnp.where(lax.bitwise_and(k, lon - 1) == want, 1.0, 0.0).astype(BF16)

    def sigma(s, width):
        at = lvl[0] - s
        now = jnp.full((1, width), plan[jnp.maximum(at, 0)], F32)
        after = jnp.full((1, width), plan[jnp.maximum(at - 1, 0)], F32)
        return now, after

    def in_scale_of(now):
        return 1.0 / jnp.sqrt(now * now + 1.0)

    def halo_copy(s, side):
        return pltpu.make_async_remote_copy(
            src_ref=hsend.at[s, side],
            dst_ref=hrecv.at[s, 1 - side],
            send_sem=h_ssem.at[s, side],
            recv_sem=h_rsem.at[s, 1 - side],
            device_id={"lat": lat - 1 if side == 0 else lat + 1},
            device_id_type=MESH,
        )

    def has(side):
        return lat > 0 if side == 0 else lat < n_lat - 1

    def stage_halo(s, side):
        scale = in_scale_of(sigma(s, lon)[0])
        at = 0 if side == 0 else (rows - 1) * lon
        hsend[s, side, 0:chans, :] = (cur[:, at : at + lon] * scale).astype(BF16)

    def send_halo(s, side):
        @pl.when(has(side))
        def _():
            halo_copy(s, side).start()

    base_copy = pltpu.make_async_remote_copy(
        src_ref=base_send,
        dst_ref=base_recv,
        send_sem=f_sem.at[0],
        recv_sem=f_sem.at[1],
        device_id={"hor": hor - 1},
        device_id_type=MESH,
    )
    units = [[0], [rows - 1]] + [[r, r + 1] for r in range(1, rows - 1, 2)]

    def gain_copy(u):
        part = pl.ds(units[u][0] * lon, len(units[u]) * lon)
        return pltpu.make_async_remote_copy(
            src_ref=gain_send.at[:, part],
            dst_ref=gain_recv.at[:, part],
            send_sem=g_ssem.at[u],
            recv_sem=g_rsem.at[u],
            device_id={"hor": hor - 1},
            device_id_type=MESH,
        )

    def pool_copy(s, d):
        return pltpu.make_async_remote_copy(
            src_ref=psend.at[s],
            dst_ref=precv.at[s, d - 1],
            send_sem=p_ssem.at[s, d - 1],
            recv_sem=p_rsem.at[s, d - 1],
            device_id={"hor": hor + d},
            device_id_type=MESH,
        )

    def rate_copy(d):
        return pltpu.make_async_remote_copy(
            src_ref=ret,
            dst_ref=rrecv.at[d - 1],
            send_sem=r_ssem.at[d - 1],
            recv_sem=r_rsem.at[d - 1],
            device_id={"hor": hor + d},
            device_id_type=MESH,
        )

    def lift(scaled, sm, sh):
        return silu(dot(liftw[...], scaled) * sm + sh).astype(F32)

    def place(feat, block):
        at = block * lon
        low = feat.astype(BF16)
        stack[0:hidden, at : at + lon] = pltpu.roll(feat, 1, 1).astype(BF16)
        stack[hidden : 2 * hidden, at : at + lon] = low
        stack[2 * hidden : 3 * hidden, at : at + lon] = pltpu.roll(feat, lon - 1, 1).astype(BF16)

    loads[0].wait()
    for row in range(rows):
        cur[:, row * lon : (row + 1) * lon] = win[pl.ds(row, chans, stride=rows), :]
    for side in range(2):
        stage_halo(0, side)
    n_near = jnp.where(lat > 0, 1, 0) + jnp.where(lat < n_lat - 1, 1, 0)
    pl.semaphore_wait(barrier, n_near + (n_hor - 1))
    for side in range(2):
        send_halo(0, side)
    for load in loads[1:5]:
        load.wait()
    mods[0] = jnp.broadcast_to(column(msc[...], 0, hidden), (hidden, lon))
    mods[1] = jnp.broadcast_to(column(msh[...], 0, hidden), (hidden, lon))
    eye = (
        lax.broadcasted_iota(jnp.int32, (chans, chans), 0)
        == lax.broadcasted_iota(jnp.int32, (chans, chans), 1)
    ).astype(F32).astype(BF16)
    liftw[...] = lax.dot_general(
        liftt[...], eye, (((0,), (0,)), ((), ())), preferred_element_type=F32
    ).astype(BF16)
    for d in range(1, n_hor):

        @pl.when(hor + d < n_hor)
        def _():
            rate_copy(d).start()

    for load in loads[5:]:
        load.wait()

    @pl.loop(0, STEPS)
    def _(s):
        now, after = sigma(s, lon)
        scale = in_scale_of(now)
        log_sigma = jnp.log(now)
        ratio = after / now
        keep = ratio + (1.0 - ratio) / (now * now + 1.0)
        gain = (1.0 - ratio) * (now * scale)

        @pl.when((s == STEPS - 1) & (hor > 0))
        def _():
            for row in range(rows):
                at = row * lon
                base_send[:, at : at + lon] = keep * cur[:, at : at + lon]
            base_copy.start()

        sm = 1.0 + log_sigma * mods[0]
        sh = log_sigma * mods[1]
        for p in range(n_pairs):
            scaled = jnp.concatenate(
                [
                    (cur[:, (2 * p + i) * lon : (2 * p + i + 1) * lon] * scale).astype(BF16)
                    for i in range(2)
                ],
                axis=1,
            )
            lifted = dot(liftw[...], scaled)
            for i in range(2):
                place(silu(lifted[:, i * lon : (i + 1) * lon] * sm + sh), 2 * p + i + 1)
        pooled = jnp.zeros((half, lon), F32)
        for p in range(n_pairs):
            tok = 2 * p // POOL
            for side in range(2):
                k0 = hidden + side * half
                feat = stack[k0 : k0 + half, (2 * p + 1) * lon : (2 * p + 3) * lon]
                pooled = pooled + dot(feat, poolm[2 * tok + side])
        psend[s] = pooled.astype(WIRE)
        for d in range(1, n_hor):

            @pl.when(hor + d < n_hor)
            def _():
                pool_copy(s, d).start()

        ctx[...] = pooled
        for p in range(n_pairs):
            total = dot(convw[1], stack[:, (2 * p + 1) * lon : (2 * p + 3) * lon])
            if p > 0:
                total = total + dot(convw[0], stack[:, 2 * p * lon : (2 * p + 2) * lon])
            if p < n_pairs - 1:
                total = total + dot(convw[2], stack[:, (2 * p + 2) * lon : (2 * p + 4) * lon])
            acc[:, p * pair : (p + 1) * pair] = total
        acc[:, lon:pair] += dot(convw[0], stack[:, lon:pair])
        last = (rows - 1) * lon
        acc[:, last - lon : last] += dot(convw[2], stack[:, rows * lon : (rows + 1) * lon])

        @pl.when(s == 0)
        def _():
            coef[0] = packed_rate(ret[...])
            for d in range(1, n_hor):

                @pl.when(hor >= d)
                def _():
                    rate_copy(d).wait_recv()
                    if d < n_hor - 1:
                        coef[d] = coef[d - 1] * packed_rate(rrecv[d - 1])

        for d in range(1, n_hor):

            @pl.when(hor >= d)
            def _():
                pool_copy(s, d).wait_recv()
                ctx[...] += coef[d - 1] * precv[s, d - 1].astype(F32)

        total = ctx[...]
        high = total.astype(BF16)
        low = (total - high.astype(F32)).astype(BF16)
        both = jnp.concatenate([high, low], axis=1)
        up[0:half, :] = dot(both, spread[0])
        up[half:hidden, :] = dot(both, spread[1])

        def finish(u):
            unit = units[u]
            gated = []
            for row in unit:
                at = row * lon
                tok = row // POOL
                ctx_up = up[:, tok * lon : (tok + 1) * lon]
                feat = stack[hidden : 2 * hidden, at + lon : at + 2 * lon].astype(F32)
                gated.append(silu(feat + acc[:, at : at + lon] + ctx_up).astype(BF16))
            gated = gated[0] if len(gated) == 1 else jnp.concatenate(gated, axis=1)
            outputs = dot(outw[...], gated)
            for i, row in enumerate(unit):
                at = row * lon
                step = gain * outputs[:, i * lon : (i + 1) * lon]
                cur[:, at : at + lon] = keep * cur[:, at : at + lon] + step
                gain_send[0:chans, at : at + lon] = step.astype(BF16)
            if u < 2:

                @pl.when(s < STEPS - 1)
                def _():
                    stage_halo(s + 1, u)
                    send_halo(s + 1, u)

            @pl.when((s == STEPS - 1) & (hor > 0))
            def _():
                gain_copy(u).start()

        for u in range(2, len(units)):
            finish(u)

        for side in range(2):

            @pl.when(has(side))
            def _():
                halo_copy(s, 1 - side).wait_recv()

        near = jnp.concatenate([hrecv[s, side, 0:chans, :] for side in range(2)], axis=1)
        near = dot(liftw[...], near)
        for side in range(2):
            feat = silu(near[:, side * lon : (side + 1) * lon] * sm + sh)
            block = 0 if side == 0 else rows + 1
            place(jnp.where(has(side), feat, 0.0), block)
            at = 0 if side == 0 else last
            acc[:, at : at + lon] += dot(
                convw[2 * side], stack[:, block * lon : (block + 1) * lon]
            )

        finish(0)
        finish(1)

    for row in range(rows):
        wout[pl.ds(row, chans, stride=rows), :] = cur[:, row * lon : (row + 1) * lon]

    @pl.when(hor == n_hor - 1)
    def _():
        fresh_load.wait()
        arr[...] = plan[plan.shape[0] - 1] * arr[...]

    @pl.when(hor < n_hor - 1)
    def _():
        base_copy.wait_recv()
        for u in range(len(units)):
            gain_copy(u).wait_recv()
            for row in units[u]:
                at = row * lon
                arr[pl.ds(row, chans, stride=rows), :] = base_recv[:, at : at + lon] + gain_recv[
                    0:chans, at : at + lon
                ].astype(F32)

    for d in range(1, n_hor):

        @pl.when(hor + d < n_hor)
        def _():
            rate_copy(d).wait_send()
            for s in range(STEPS):
                pool_copy(s, d).wait_send()

    for s in range(STEPS):
        for side in range(2):

            @pl.when(has(side))
            def _():
                halo_copy(s, side).wait_send()

    @pl.when(hor > 0)
    def _():
        base_copy.wait_send()
        for u in range(len(units)):
            gain_copy(u).wait_send()


def write(a, b, a_out, b_out, sem):
    copies = [pltpu.make_async_copy(x, y, sem.at[i]) for i, (x, y) in enumerate([(a, a_out), (b, b_out)])]
    for copy in copies:
        copy.start()
    for copy in copies:
        copy.wait()


def body(
    n_hor,
    n_lat,
    window,
    fresh_noise,
    level_index,
    plan,
    retention,
    lift_weight,
    mod_scale,
    mod_shift,
    conv_weight,
    out_weight,
):
    frames, chans, rows, lon = window.shape
    hidden = conv_weight.shape[1]
    half = hidden // 2
    cells = rows * lon
    cpad = -(-chans // 16) * 16
    peers = max(1, n_hor - 1)
    vmem = pl.BlockSpec(memory_space=pltpu.VMEM)
    hbm = pl.BlockSpec(memory_space=pltpu.HBM)
    smem = pl.BlockSpec(memory_space=pltpu.SMEM)
    flat = jax.ShapeDtypeStruct((chans * rows, lon), F32)
    dma = pltpu.SemaphoreType.DMA
    current, arriving = pl.pallas_call(
        functools.partial(kernel, rows, lon, n_hor, n_lat),
        out_shape=(pltpu.VMEM(flat.shape, F32), pltpu.VMEM(flat.shape, F32)),
        in_specs=[smem, smem] + [hbm] * 8,
        out_specs=(vmem, vmem),
        scratch_shapes=[
            pltpu.VMEM((chans * rows, lon), F32),
            pltpu.VMEM((1, hidden), F32),
            pltpu.VMEM((1, hidden), F32),
            pltpu.VMEM((1, hidden), F32),
            pltpu.VMEM((chans, hidden), BF16),
            pltpu.VMEM(conv_weight.shape, BF16),
            pltpu.VMEM((chans, hidden), BF16),
            pltpu.VMEM((hidden, chans), BF16),
            pltpu.VMEM((chans, cells), F32),
            pltpu.VMEM((chans, cells), F32),
            pltpu.VMEM((cpad, cells), BF16),
            pltpu.VMEM((cpad, cells), BF16),
            pltpu.VMEM((chans, cells), F32),
            pltpu.VMEM((3 * hidden, cells + 2 * lon), BF16),
            pltpu.VMEM((hidden, cells), F32),
            pltpu.VMEM((hidden, 2 * lon), F32),
            pltpu.VMEM((peers, half, lon), F32),
            pltpu.VMEM((2, hidden, lon), F32),
            pltpu.VMEM((2 * (rows // POOL), 2 * lon, lon), BF16),
            pltpu.VMEM((2, 2 * lon, 2 * lon), BF16),
            pltpu.VMEM((half, lon), F32),
            pltpu.VMEM((STEPS, 2, cpad, lon), BF16),
            pltpu.VMEM((STEPS, 2, cpad, lon), BF16),
            pltpu.VMEM((STEPS, half, lon), WIRE),
            pltpu.VMEM((STEPS, peers, half, lon), WIRE),
            pltpu.VMEM((peers, 1, hidden), F32),
            dma((STEPS, 2)),
            dma((STEPS, 2)),
            dma((STEPS, peers)),
            dma((STEPS, peers)),
            dma((peers,)),
            dma((peers,)),
            dma((8,)),
            dma((2,)),
            dma((rows,)),
            dma((rows,)),
        ],
        compiler_params=pltpu.CompilerParams(
            collective_id=0, has_side_effects=True, vmem_limit_bytes=66400000
        ),
    )(
        level_index,
        plan,
        window.reshape(chans * rows, lon),
        fresh_noise.reshape(chans * rows, lon),
        retention,
        mod_scale.reshape(1, hidden),
        mod_shift.reshape(1, hidden),
        lift_weight.T,
        conv_weight,
        out_weight,
    )
    shape = (frames, chans, rows, lon)
    current, rolled = pl.pallas_call(
        write,
        out_shape=(flat, flat),
        in_specs=[vmem, vmem],
        out_specs=(hbm, hbm),
        scratch_shapes=[dma((2,))],
        compiler_params=pltpu.CompilerParams(vmem_limit_bytes=4 * 1024 * 1024),
    )(current, arriving)
    return (current.reshape(shape), rolled.reshape(shape))


def solution(mesh):
    in_specs = (
        P("hor", None, "lat", None),
        P(None, "lat", None),
        P("hor"),
        P(),
        P("hor", None),
        P(),
        P(),
        P(),
        P(),
        P(),
    )
    out_specs = (P("hor", None, "lat", None), P("hor", None, "lat", None))
    run = functools.partial(body, mesh.shape["hor"], mesh.shape["lat"])
    return jax.shard_map(run, mesh=mesh, in_specs=in_specs, out_specs=out_specs, check_vma=False)
```

profile of v0, /device:TPU:1, one launch (start us, length us, event | category | flops | bytes accessed | tf_op | source)
XLA Modules:
  0.0 22.5 jit_solution(14435786494445284671)
XLA Ops:
  1.3 20.4 %shard_map.113 = (f32[552,128]{1,0:T(8,128)S(1)}, f32[552,128]{1,0:T(8,128)S(1)}) custom-call(s32[1]{0:T(128)S(6)} %copy.12.lvl, f32[64]{0:T(128)} %plan.1, f32[552,128]{1,0:T(8,128)} %bitcast.7, f32[552,128]{1,0:T(8,128)} %bitcast.8, f32[1,192]{1,0:T(1,128)} %ret_h.1, f32[1,192]{1,0:T(1,128)} %bitcast.10, f32[1,192]{1,0:T(1,128)} %bitcast.11, ...), custom_call_target="tpu_custom_call" | custom-call | tf_op jit(solution)/shard_map/pallas_call | solution.py:462
  21.7 0.8 %shard_map.114 = (f32[552,128]{1,0:T(8,128)}, f32[552,128]{1,0:T(8,128)}) custom-call(f32[552,128]{1,0:T(8,128)S(1)} %get-tuple-element.6.a, f32[552,128]{1,0:T(8,128)S(1)} %get-tuple-element.7.b), custom_call_target="tpu_custom_call" | custom-call | tf_op jit(solution)/shard_map/pallas_call | solution.py:521
where the time goes:
time: 22.7 us; the launch traced here: 22.5 us
  Pallas kernels  21.3 us (94%)
  between operations  1.29 us (6%)
    pallas_call x1, Pallas kernels, body(): pl.pallas_call(functools.partial(kernel, rows, lon, n_hor, n_lat), out_sh...  20.4 us
    pallas_call x1, Pallas kernels, body(): pl.pallas_call(write, out_shape=(flat, flat), in_specs=[vmem, vmem], out_...  0.82 us

commit v1 on v0

v1 whole, which is shorter than its diff:
```python
import functools

import jax
import jax.numpy as jnp
from jax import lax
from jax.experimental import pallas as pl
from jax.experimental.pallas import tpu as pltpu
from jax.sharding import PartitionSpec as P

POOL = 4
STEPS = 3
MESH = pl.DeviceIdType.MESH
F32 = jnp.float32
BF16 = jnp.bfloat16
WIRE = jnp.bfloat16


def dot(a, b):
    return jnp.dot(a, b, preferred_element_type=F32)


def kernel(
    rows,
    lon,
    n_hor,
    n_lat,
    lvl_h,
    plan_h,
    win_h,
    fresh_h,
    ret_h,
    msc_h,
    msh_h,
    lift_h,
    convw_h,
    outw_h,
    wout,
    arr,
    lvl,
    plan,
    win,
    ret,
    msc,
    msh,
    liftt,
    convw,
    outw,
    liftw,
    taps,
    base_send,
    base_recv,
    rest_send,
    rest_recv,
    cur,
    stack,
    acc,
    up,
    coef,
    mods,
    smsh,
    poolm,
    spread,
    ctx,
    hsend,
    hrecv,
    psend,
    precv,
    rrecv,
    h_ssem,
    h_rsem,
    p_ssem,
    p_rsem,
    r_ssem,
    r_rsem,
    l_sem,
    f_sem,
):
    hidden, chans = liftw.shape
    half = hidden // 2
    n_pairs = rows // 2
    hor = lax.axis_index("hor")
    lat = lax.axis_index("lat")

    barrier = pltpu.get_barrier_semaphore()

    @pl.when(lat > 0)
    def _():
        pl.semaphore_signal(barrier, inc=1, device_id={"lat": lat - 1}, device_id_type=MESH)

    @pl.when(lat < n_lat - 1)
    def _():
        pl.semaphore_signal(barrier, inc=1, device_id={"lat": lat + 1}, device_id_type=MESH)

    for d in range(1, n_hor):
        pl.semaphore_signal(
            barrier, inc=1, device_id={"hor": lax.rem(hor + d, n_hor)}, device_id_type=MESH
        )

    pairs = [(win_h, win), (lvl_h, lvl), (plan_h, plan)]
    pairs += [(msc_h, msc), (msh_h, msh), (ret_h, ret), (lift_h, liftt)]
    pairs += [(convw_h, convw), (outw_h, outw)]
    loads = [pltpu.make_async_copy(a, b, l_sem.at[i]) for i, (a, b) in enumerate(pairs)]
    fresh_load = pltpu.make_async_copy(fresh_h, arr, l_sem.at[len(pairs)])
    for load in loads:
        load.start()

    @pl.when(hor == n_hor - 1)
    def _():
        fresh_load.start()

    def has(side):
        low, high = lat > 0, lat < n_lat - 1
        if isinstance(side, int):
            return low if side == 0 else high
        return jnp.logical_or(
            jnp.logical_and(side == 0, low), jnp.logical_and(side == 1, high)
        )

    for side in range(2):

        @pl.when(jnp.logical_not(has(side)))
        def _():
            hrecv[:, side] = jnp.zeros_like(hrecv[:, side])

    stack[0] = jnp.zeros_like(stack[0])
    stack[rows + 1] = jnp.zeros_like(stack[rows + 1])

    def column(row_ref_value, start, count):
        sub = lax.broadcasted_iota(jnp.int32, (count, hidden), 0) + start
        lane = lax.broadcasted_iota(jnp.int32, (count, hidden), 1)
        return jnp.sum(jnp.where(sub == lane, row_ref_value, 0.0), axis=1, keepdims=True)

    def packed_rate(value):
        lane = lax.broadcasted_iota(jnp.int32, (half, lon), 1)
        lo = jnp.broadcast_to(column(value, 0, half), (half, lon))
        hi = jnp.broadcast_to(column(value, half, half), (half, lon))
        return jnp.where(lane < lon // 2, lo, hi)

    groups = lon // POOL
    k = lax.broadcasted_iota(jnp.int32, (rows * lon, lon), 0)
    n = lax.broadcasted_iota(jnp.int32, (rows * lon, lon), 1)
    shift = POOL.bit_length() - 1
    row_of = lax.shift_right_logical(k, lon.bit_length() - 1)
    want = lax.shift_right_logical(row_of, shift) * groups + lax.shift_right_logical(
        lax.bitwise_and(k, lon - 1), shift
    )
    poolm[...] = jnp.where(want == n, 1.0 / (POOL * POOL), 0.0).astype(BF16)
    for side in range(2):
        k = lax.broadcasted_iota(jnp.int32, (2 * lon, 2 * lon), 0)
        n = lax.broadcasted_iota(jnp.int32, (2 * lon, 2 * lon), 1)
        want = side * (lon // 2) + lax.shift_right_logical(n, shift)
        spread[side] = jnp.where(lax.bitwise_and(k, lon - 1) == want, 1.0, 0.0).astype(BF16)

    def sigma(s, width):
        at = lvl[0] - s
        now = jnp.full((1, width), plan[jnp.maximum(at, 0)], F32)
        after = jnp.full((1, width), plan[jnp.maximum(at - 1, 0)], F32)
        return now, after

    def in_scale_of(now):
        return 1.0 / jnp.sqrt(now * now + 1.0)

    def halo_copy(s, side):
        return pltpu.make_async_remote_copy(
            src_ref=hsend.at[s, side],
            dst_ref=hrecv.at[s, 1 - side],
            send_sem=h_ssem.at[s, side],
            recv_sem=h_rsem.at[s, 1 - side],
            device_id={"lat": lat - 1 + 2 * side},
            device_id_type=MESH,
        )

    def send_halo(s, side):
        @pl.when(has(side))
        def _():
            halo_copy(s, side).start()

    back = {"hor": hor - 1}
    base_copy = pltpu.make_async_remote_copy(
        src_ref=base_send,
        dst_ref=base_recv,
        send_sem=f_sem.at[0],
        recv_sem=f_sem.at[1],
        device_id=back,
        device_id_type=MESH,
    )

    def rest_copy(u):
        part = pl.ds(0 if u == 0 else rows - 1 if u == 1 else 1, 1 if u < 2 else rows - 2)
        return pltpu.make_async_remote_copy(
            src_ref=rest_send.at[part],
            dst_ref=rest_recv.at[part],
            send_sem=f_sem.at[2 + u],
            recv_sem=f_sem.at[5 + u],
            device_id=back,
            device_id_type=MESH,
        )

    def pool_copy(s, d):
        return pltpu.make_async_remote_copy(
            src_ref=psend.at[s],
            dst_ref=precv.at[s, d - 1],
            send_sem=p_ssem.at[s, d - 1],
            recv_sem=p_rsem.at[s, d - 1],
            device_id={"hor": hor + d},
            device_id_type=MESH,
        )

    def rate_copy(d):
        return pltpu.make_async_remote_copy(
            src_ref=ret,
            dst_ref=rrecv.at[d - 1],
            send_sem=r_ssem.at[d - 1],
            recv_sem=r_rsem.at[d - 1],
            device_id={"hor": hor + d},
            device_id_type=MESH,
        )

    def half_silu(h):
        return h + h * jnp.tanh(h)

    def wide(ref, first):
        return jnp.concatenate([ref[first], ref[first + 1]], axis=1)

    def shifted(feat):
        low = feat.astype(BF16)
        ahead = pltpu.roll(feat, 1, 1).astype(BF16)
        behind = pltpu.roll(feat, lon - 1, 1).astype(BF16)
        return ahead, low, behind

    def place(feat, block):
        for b, part in enumerate(shifted(feat)):
            stack[block, b * hidden : (b + 1) * hidden, :] = part

    for load in loads[0:3]:
        load.wait()
    scale = in_scale_of(sigma(0, lon)[0])
    for side, row in enumerate((0, rows - 1)):
        edge_row = win[pl.ds(row, chans, stride=rows), :]
        hsend[0, side, 0:chans, :] = (edge_row * scale).astype(BF16)
    n_near = jnp.where(lat > 0, 1, 0) + jnp.where(lat < n_lat - 1, 1, 0)
    pl.semaphore_wait(barrier, n_near + (n_hor - 1))
    for side in range(2):
        send_halo(0, side)
    for load in loads[3:7]:
        load.wait()
    for d in range(1, n_hor):

        @pl.when(hor + d < n_hor)
        def _():
            rate_copy(d).start()

    for row in range(rows):
        cur[row] = win[pl.ds(row, chans, stride=rows), :]
    mods[0] = jnp.broadcast_to(column(msc[...], 0, hidden), (hidden, lon))
    mods[1] = jnp.broadcast_to(column(msh[...], 0, hidden), (hidden, lon))
    eye = (
        lax.broadcasted_iota(jnp.int32, (chans, chans), 0)
        == lax.broadcasted_iota(jnp.int32, (chans, chans), 1)
    ).astype(F32).astype(BF16)
    liftw[...] = lax.dot_general(
        liftt[...], eye, (((0,), (0,)), ((), ())), preferred_element_type=F32
    ).astype(BF16)

    for load in loads[7:]:
        load.wait()
    taps[...] = jnp.concatenate([convw[a] for a in range(3)], axis=1)

    @pl.loop(0, STEPS)
    def _(s):
        now, after = sigma(s, lon)
        scale = in_scale_of(now)
        log_sigma = jnp.log(now)
        ratio = after / now
        keep = ratio + (1.0 - ratio) / (now * now + 1.0)
        gain = (1.0 - ratio) * (now * scale)
        scale_next = in_scale_of(after)

        @pl.when((s == STEPS - 1) & (hor > 0))
        def _():
            for row in range(rows):
                base_send[row, 0:chans, :] = (keep * cur[row]).astype(BF16)
            base_copy.start()

        smsh[0] = 0.5 * (1.0 + log_sigma * mods[0])
        smsh[1] = 0.5 * (log_sigma * mods[1])
        for p in range(n_pairs):
            scaled = jnp.concatenate(
                [(cur[2 * p + i] * scale).astype(BF16) for i in range(2)], axis=1
            )
            lifted = dot(liftw[...], scaled)
            for i in range(2):
                h = lifted[:, i * lon : (i + 1) * lon] * smsh[0] + smsh[1]
                place(half_silu(h), 2 * p + i + 1)
        flat = jnp.concatenate(
            [stack[row + 1, hidden : 2 * hidden, :] for row in range(rows)], axis=1
        )
        pooled = dot(flat, poolm[...])
        pooled = pooled[0:half] + pltpu.roll(pooled[half:hidden], lon // 2, 1)
        psend[s] = pooled.astype(WIRE)
        for d in range(1, n_hor):

            @pl.when(hor + d < n_hor)
            def _():
                pool_copy(s, d).start()

        ctx[...] = pooled
        for p in range(n_pairs):
            rhs = jnp.concatenate([wide(stack, 2 * p + a) for a in range(3)], axis=0)
            total = dot(taps[...], rhs)
            for i in range(2):
                acc[2 * p + i] = total[:, i * lon : (i + 1) * lon]

        @pl.when(s == 0)
        def _():
            coef[0] = packed_rate(ret[...])
            for d in range(1, n_hor):

                @pl.when(hor >= d)
                def _():
                    rate_copy(d).wait_recv()
                    if d < n_hor - 1:
                        coef[d] = coef[d - 1] * packed_rate(rrecv[d - 1])

        for d in range(1, n_hor):

            @pl.when(hor >= d)
            def _():
                pool_copy(s, d).wait_recv()
                ctx[...] += coef[d - 1] * precv[s, d - 1].astype(F32)

        total = ctx[...]
        high = total.astype(BF16)
        low = (total - high.astype(F32)).astype(BF16)
        both = jnp.concatenate([high, low], axis=1)
        for side in range(2):
            spread_up = dot(both, spread[side])
            for tok in range(2):
                up[tok, side * half : (side + 1) * half, :] = spread_up[:, tok * lon : (tok + 1) * lon]

        def gate(row, extra, tok):
            feat = stack[row + 1, hidden : 2 * hidden, :].astype(F32)
            h = 0.5 * (feat + extra + up[tok])
            return half_silu(h).astype(BF16)

        def advance(row, outputs):
            nxt = keep * cur[row] + gain * outputs
            cur[row] = nxt
            rest_send[row, 0:chans, :] = (nxt - base_send[row, 0:chans, :].astype(F32)).astype(BF16)
            return nxt

        def finish_inner():
            for first in range(1, rows - 1, 2):
                gated = jnp.concatenate(
                    [gate(row, acc[row], row // POOL) for row in (first, first + 1)], axis=1
                )
                outputs = dot(outw[...], gated)
                for i in range(2):
                    advance(first + i, outputs[:, i * lon : (i + 1) * lon])

            @pl.when((s == STEPS - 1) & (hor > 0))
            def _():
                rest_copy(2).start()

        early = (hor < 2) | (s == STEPS - 1)

        @pl.when(early)
        def _():
            finish_inner()

        def wait_edges():
            for side in range(2):

                @pl.when(has(side))
                def _():
                    halo_copy(s, 1 - side).wait_recv()

        def finish_edges():
            near = jnp.concatenate([hrecv[s, side, 0:chans, :] for side in range(2)], axis=1)
            near = dot(liftw[...], near)
            gated = []
            for side, row in enumerate((0, rows - 1)):
                h = near[:, side * lon : (side + 1) * lon] * smsh[0] + smsh[1]
                feat = jnp.where(has(side), half_silu(h), 0.0)
                extra = acc[row] + dot(convw[2 * side], jnp.concatenate(shifted(feat), axis=0))
                gated.append(gate(row, extra, row // POOL))
            outputs = dot(outw[...], jnp.concatenate(gated, axis=1))
            later = s + 1
            for side, row in enumerate((0, rows - 1)):
                nxt = advance(row, outputs[:, side * lon : (side + 1) * lon])
                hsend[later, side, 0:chans, :] = (nxt * scale_next).astype(BF16)

        def send_edges():
            for side in range(2):

                @pl.when((s < STEPS - 1) & has(side))
                def _():
                    halo_copy(s + 1, side).start()

        wait_edges()
        finish_edges()
        send_edges()

        @pl.when((s == STEPS - 1) & (hor > 0))
        def _():
            for u in range(2):
                rest_copy(u).start()

        @pl.when(jnp.logical_not(early))
        def _():
            finish_inner()

    for row in range(rows):
        wout[pl.ds(row, chans, stride=rows), :] = cur[row]

    @pl.when(hor == n_hor - 1)
    def _():
        fresh_load.wait()
        arr[...] = plan[plan.shape[0] - 1] * arr[...]

    @pl.when(hor < n_hor - 1)
    def _():
        base_copy.wait_recv()
        for u, unit in ((2, range(1, rows - 1)), (0, [0]), (1, [rows - 1])):
            rest_copy(u).wait_recv()
            for row in unit:
                arr[pl.ds(row, chans, stride=rows), :] = base_recv[row, 0:chans, :].astype(
                    F32
                ) + rest_recv[row, 0:chans, :].astype(F32)

    for d in range(1, n_hor):

        @pl.when(hor + d < n_hor)
        def _():
            rate_copy(d).wait_send()
            for s in range(STEPS):
                pool_copy(s, d).wait_send()

    for s in range(STEPS):
        for side in range(2):

            @pl.when(has(side))
            def _():
                halo_copy(s, side).wait_send()

    @pl.when(hor > 0)
    def _():
        base_copy.wait_send()
        for u in range(3):
            rest_copy(u).wait_send()


def write(a, b, a_out, b_out, sem):
    copies = [pltpu.make_async_copy(x, y, sem.at[i]) for i, (x, y) in enumerate([(a, a_out), (b, b_out)])]
    for copy in copies:
        copy.start()
    for copy in copies:
        copy.wait()


def body(
    n_hor,
    n_lat,
    window,
    fresh_noise,
    level_index,
    plan,
    retention,
    lift_weight,
    mod_scale,
    mod_shift,
    conv_weight,
    out_weight,
):
    frames, chans, rows, lon = window.shape
    hidden = conv_weight.shape[1]
    half = hidden // 2
    cpad = -(-chans // 16) * 16
    peers = max(1, n_hor - 1)
    vmem = pl.BlockSpec(memory_space=pltpu.VMEM)
    hbm = pl.BlockSpec(memory_space=pltpu.HBM)
    flat = jax.ShapeDtypeStruct((chans * rows, lon), F32)
    dma = pltpu.SemaphoreType.DMA
    current, arriving = pl.pallas_call(
        functools.partial(kernel, rows, lon, n_hor, n_lat),
        out_shape=(pltpu.VMEM(flat.shape, F32), pltpu.VMEM(flat.shape, F32)),
        in_specs=[hbm] * 10,
        out_specs=(vmem, vmem),
        scratch_shapes=[
            pltpu.SMEM(level_index.shape, jnp.int32),
            pltpu.SMEM(plan.shape, F32),
            pltpu.VMEM((chans * rows, lon), F32),
            pltpu.VMEM((1, hidden), F32),
            pltpu.VMEM((1, hidden), F32),
            pltpu.VMEM((1, hidden), F32),
            pltpu.VMEM((chans, hidden), BF16),
            pltpu.VMEM(conv_weight.shape, BF16),
            pltpu.VMEM((chans, hidden), BF16),
            pltpu.VMEM((hidden, chans), BF16),
            pltpu.VMEM((hidden, 9 * hidden), BF16),
            pltpu.VMEM((rows, cpad, lon), BF16),
            pltpu.VMEM((rows, cpad, lon), BF16),
            pltpu.VMEM((rows, cpad, lon), BF16),
            pltpu.VMEM((rows, cpad, lon), BF16),
            pltpu.VMEM((rows, chans, lon), F32),
            pltpu.VMEM((rows + 2, 3 * hidden, lon), BF16),
            pltpu.VMEM((rows, hidden, lon), F32),
            pltpu.VMEM((rows // POOL, hidden, lon), F32),
            pltpu.VMEM((peers, half, lon), F32),
            pltpu.VMEM((2, hidden, lon), F32),
            pltpu.VMEM((2, hidden, lon), F32),
            pltpu.VMEM((rows * lon, lon), BF16),
            pltpu.VMEM((2, 2 * lon, 2 * lon), BF16),
            pltpu.VMEM((half, lon), F32),
            pltpu.VMEM((STEPS + 1, 2, cpad, lon), BF16),
            pltpu.VMEM((STEPS, 2, cpad, lon), BF16),
            pltpu.VMEM((STEPS, half, lon), WIRE),
            pltpu.VMEM((STEPS, peers, half, lon), WIRE),
            pltpu.VMEM((peers, 1, hidden), F32),
            dma((STEPS, 2)),
            dma((STEPS, 2)),
            dma((STEPS, peers)),
            dma((STEPS, peers)),
            dma((peers,)),
            dma((peers,)),
            dma((10,)),
            dma((8,)),
        ],
        compiler_params=pltpu.CompilerParams(
            collective_id=0, has_side_effects=True, vmem_limit_bytes=66400000
        ),
    )(
        level_index,
        plan,
        window.reshape(chans * rows, lon),
        fresh_noise.reshape(chans * rows, lon),
        retention,
        mod_scale.reshape(1, hidden),
        mod_shift.reshape(1, hidden),
        lift_weight.T,
        conv_weight,
        out_weight,
    )
    shape = (frames, chans, rows, lon)
    current, rolled = pl.pallas_call(
        write,
        out_shape=(flat, flat),
        in_specs=[vmem, vmem],
        out_specs=(hbm, hbm),
        scratch_shapes=[dma((2,))],
        compiler_params=pltpu.CompilerParams(vmem_limit_bytes=4 * 1024 * 1024),
    )(current, arriving)
    return (current.reshape(shape), rolled.reshape(shape))


def solution(mesh):
    in_specs = (
        P("hor", None, "lat", None),
        P(None, "lat", None),
        P("hor"),
        P(),
        P("hor", None),
        P(),
        P(),
        P(),
        P(),
        P(),
    )
    out_specs = (P("hor", None, "lat", None), P("hor", None, "lat", None))
    run = functools.partial(body, mesh.shape["hor"], mesh.shape["lat"])
    return jax.shard_map(run, mesh=mesh, in_specs=in_specs, out_specs=out_specs, check_vma=False)
```

time: 22.7 us -> 21.3 us (0.938)
  Pallas kernels: 21.3 us -> 19.9 us
    pallas_call x1, Pallas kernels: 20.4 us -> 19.1 us  [body(): pl.pallas_call(functools.partial(kernel, rows, lon, n_hor, n_lat), out_sh...]
where the time goes in v1:
time: 21.3 us; the launch traced here: 21.2 us
  Pallas kernels  19.9 us (93%)
  between operations  1.29 us (6%)
    pallas_call x1, Pallas kernels, body(): pl.pallas_call(functools.partial(kernel, rows, lon, n_hor, n_lat), out_sh...  19.1 us
    pallas_call x1, Pallas kernels, body(): pl.pallas_call(write, out_shape=(flat, flat), in_specs=[vmem, vmem], out_...  0.82 us

profile of v1, /device:TPU:1, one launch (start us, length us, event | category | flops | bytes accessed | tf_op | source)
XLA Modules:
  0.0 21.2 jit_solution(16345761359871792239)
XLA Ops:
  1.3 19.1 %shard_map.113 = (f32[552,128]{1,0:T(8,128)S(1)}, f32[552,128]{1,0:T(8,128)S(1)}) custom-call(s32[1]{0:T(128)S(6)} %copy.12.lvl_h, f32[64]{0:T(128)} %plan_h.1, f32[552,128]{1,0:T(8,128)} %bitcast.7, f32[552,128]{1,0:T(8,128)} %bitcast.8, f32[1,192]{1,0:T(1,128)} %ret_h.1, f32[1,192]{1,0:T(1,128)} %bitcast.10, f32[1,192]{1,0:T(1,128)} %bitcast.11, ...), custom_call_target="tpu_custom_call" | custom-call | tf_op jit(solution)/shard_map/pallas_call | solution.py:484
  20.3 0.8 %shard_map.114 = (f32[552,128]{1,0:T(8,128)}, f32[552,128]{1,0:T(8,128)}) custom-call(f32[552,128]{1,0:T(8,128)S(1)} %get-tuple-element.6.a, f32[552,128]{1,0:T(8,128)S(1)} %get-tuple-element.7.b), custom_call_target="tpu_custom_call" | custom-call | tf_op jit(solution)/shard_map/pallas_call | solution.py:545

commit v2 on v1

v2 whole, which is shorter than its diff:
```python
import functools

import jax
import jax.numpy as jnp
from jax import lax
from jax.experimental import pallas as pl
from jax.experimental.pallas import tpu as pltpu
from jax.sharding import PartitionSpec as P

POOL = 4
STEPS = 3
MESH = pl.DeviceIdType.MESH
F32 = jnp.float32
BF16 = jnp.bfloat16
WIRE = jnp.bfloat16


def dot(a, b):
    return jnp.dot(a, b, preferred_element_type=F32)


def kernel(
    rows,
    lon,
    n_hor,
    n_lat,
    lvl_h,
    plan_h,
    win_h,
    fresh_h,
    ret_h,
    msc_h,
    msh_h,
    lift_h,
    convw_h,
    outw_h,
    wout,
    arr,
    lvl,
    plan,
    win,
    rets,
    rfar,
    msc,
    msh,
    liftt,
    convw,
    outw,
    liftw,
    taps,
    home,
    feats0,
    csend,
    xsend,
    xrecv,
    cur,
    stack,
    fsend,
    frecv,
    acc,
    up,
    mods,
    smsh,
    sig,
    poolm,
    spread,
    rate,
    coef,
    far,
    hsend,
    hrecv,
    psend,
    precv,
    qsend,
    qrecv,
    base_send,
    base_recv,
    rest_send,
    rest_recv,
    fin_recv,
    l_sem,
    c_sem,
    g_sem,
    h_sem,
    h0_sem,
    f_sem,
    p_sem,
    q_ssem,
    q_rsem,
    rf_ssem,
    rf_rsem,
    r_ssem,
    r_rsem,
    e_sem,
):
    hidden, chans = liftw.shape
    half = hidden // 2
    n_chip = n_hor // 2
    hor = lax.axis_index("hor")
    lat = lax.axis_index("lat")
    chip = hor // 2
    core = lax.rem(hor, 2)
    other = 1 - core
    outer = core == 1
    partner = {"hor": hor + 1 - 2 * core}
    n_near = jnp.where(lat > 0, 1, 0) + jnp.where(lat < n_lat - 1, 1, 0)

    def has(side):
        return lat > 0 if side == 0 else lat < n_lat - 1

    def remote(src, dst, ssem, rsem, where):
        return pltpu.make_async_remote_copy(
            src_ref=src,
            dst_ref=dst,
            send_sem=ssem,
            recv_sem=rsem,
            device_id=where,
            device_id_type=MESH,
        )

    barrier = pltpu.get_barrier_semaphore()

    def greet(where):
        pl.semaphore_signal(barrier, inc=1, device_id=where, device_id_type=MESH)

    for side in range(2):
        near = lat - 1 + 2 * side

        @pl.when(has(side))
        def _():
            greet({"hor": 2 * chip + 1, "lat": near})

        @pl.when(has(side) & outer)
        def _():
            greet({"hor": 2 * chip, "lat": near})

    for d in range(1, n_hor):
        greet({"hor": lax.rem(hor + d, n_hor)})

    pairs = [(win_h, win), (lvl_h, lvl), (plan_h, plan)]
    pairs += [(msc_h, msc), (msh_h, msh), (ret_h, rets.at[core]), (lift_h, liftt)]
    pairs += [(convw_h, convw), (outw_h, outw)]
    loads = [pltpu.make_async_copy(a, b, l_sem.at[i]) for i, (a, b) in enumerate(pairs)]
    fresh_load = pltpu.make_async_copy(fresh_h, arr, l_sem.at[len(pairs)])
    for load in loads:
        load.start()

    @pl.when(hor == n_hor - 1)
    def _():
        fresh_load.start()

    for side in range(2):

        @pl.when(outer & jnp.logical_not(has(side)))
        def _():
            hrecv[:, side] = jnp.zeros_like(hrecv[:, side])

    for f in range(2):
        for g in range(2):
            for block in (0, 3):
                stack[f, g, block] = jnp.zeros_like(stack[f, g, block])

    def column(row_ref_value, start, count):
        sub = lax.broadcasted_iota(jnp.int32, (count, hidden), 0) + start
        lane = lax.broadcasted_iota(jnp.int32, (count, hidden), 1)
        return jnp.sum(jnp.where(sub == lane, row_ref_value, 0.0), axis=1, keepdims=True)

    def packed_rate(value):
        lane = lax.broadcasted_iota(jnp.int32, (half, lon), 1)
        lo = jnp.broadcast_to(column(value, 0, half), (half, lon))
        hi = jnp.broadcast_to(column(value, half, half), (half, lon))
        return jnp.where(lane < lon // 2, lo, hi)

    groups = lon // POOL
    shift = POOL.bit_length() - 1
    k = lax.broadcasted_iota(jnp.int32, (4 * lon, lon), 0)
    n = lax.broadcasted_iota(jnp.int32, (4 * lon, lon), 1)
    want = lax.shift_right_logical(k, lon.bit_length()) * groups + lax.shift_right_logical(
        lax.bitwise_and(k, lon - 1), shift
    )
    poolm[...] = jnp.where(want == n, 1.0 / (POOL * POOL), 0.0).astype(BF16)
    for side in range(2):
        k = lax.broadcasted_iota(jnp.int32, (2 * lon, 2 * lon), 0)
        n = lax.broadcasted_iota(jnp.int32, (2 * lon, 2 * lon), 1)
        want = side * (lon // 2) + lax.shift_right_logical(n, shift)
        spread[side] = jnp.where(lax.bitwise_and(k, lon - 1) == want, 1.0, 0.0).astype(BF16)

    def in_scale_of(now):
        return 1.0 / jnp.sqrt(now * now + 1.0)

    def outer_row(g, r):
        return g * (rows - 2) + r

    def inner_row(g, r):
        return 2 + 2 * g + r

    def my_row(g, r):
        return jnp.where(outer, outer_row(g, r), inner_row(g, r))

    def their_row(g, r):
        return jnp.where(outer, inner_row(g, r), outer_row(g, r))

    def joint(g):
        return jnp.where(outer, 1 - g, g)

    sig_copy = remote(sig.at[core], sig.at[core], g_sem.at[0], g_sem.at[1], partner)
    ret_copy = remote(rets.at[core], rets.at[core], g_sem.at[2], g_sem.at[3], partner)
    cur_copy = remote(csend, cur.at[core], c_sem.at[0], c_sem.at[1], partner)
    x_copy = remote(xsend, xrecv, c_sem.at[2], c_sem.at[3], partner)

    def first_halo(side, f):
        return remote(
            hsend.at[0, side, f],
            hrecv.at[0, 1 - side, f],
            h0_sem.at[0, side, f],
            h0_sem.at[1, 1 - side, f],
            {"hor": 2 * chip + 1, "lat": lat - 1 + 2 * side},
        )

    def halo_copy(s, side):
        return remote(
            hsend.at[s, side],
            hrecv.at[s, 1 - side],
            h_sem.at[0, s, side],
            h_sem.at[1, s, 1 - side],
            {"lat": lat - 1 + 2 * side},
        )

    def feat_copy(s):
        return remote(fsend.at[s], frecv.at[s], f_sem.at[0, s], f_sem.at[1, s], partner)

    def pool_copy(s):
        return remote(psend.at[s], precv.at[s], p_sem.at[0, s], p_sem.at[1, s], partner)

    def far_pool_copy(s, d, to):
        return remote(
            qsend.at[s],
            qrecv.at[s, d - 1, core],
            q_ssem.at[s, d - 1, to],
            q_rsem.at[s, d - 1, core],
            {"hor": 2 * (chip + d) + to},
        )

    def far_pool_wait(s, d, c):
        return remote(
            qsend.at[s],
            qrecv.at[s, d - 1, c],
            q_ssem.at[s, d - 1, 0],
            q_rsem.at[s, d - 1, c],
            {"hor": 2 * chip + c},
        )

    def far_rate_copy(d, to, c):
        return remote(
            rets.at[core],
            rfar.at[d - 1, c],
            rf_ssem.at[d - 1, to],
            rf_rsem.at[d - 1, c],
            {"hor": 2 * (chip + d) + to},
        )

    back = {"hor": 2 * chip - 1}

    def base_copy(c):
        return remote(base_send, base_recv.at[c], r_ssem.at[0], r_rsem.at[0, c], back)

    def rest_copy(stage, c):
        return remote(
            rest_send.at[stage],
            rest_recv.at[c, stage],
            r_ssem.at[1 + stage],
            r_rsem.at[1 + stage, c],
            back,
        )

    def final_copy(f):
        return remote(cur.at[f], fin_recv.at[f], e_sem.at[0, f], e_sem.at[1, f], partner)

    def half_silu(h):
        return h + h * jnp.tanh(h)

    def shifted(feat):
        ahead = pltpu.roll(feat, 1, 1).astype(BF16)
        behind = pltpu.roll(feat, lon - 1, 1).astype(BF16)
        return jnp.concatenate([ahead, feat.astype(BF16), behind], axis=0)

    low = slice(hidden, 2 * hidden)

    def place(feat, f, g, r):
        parts = shifted(feat)
        stack[f, g, 1 + r] = parts
        if (g, r) == (0, 1):
            stack[f, 1, jnp.where(outer, 4, 0)] = parts
        if (g, r) == (1, 0):
            stack[f, 0, jnp.where(outer, 4, 3)] = parts

    def packed(value):
        return value[0:half] + pltpu.roll(value[half:hidden], lon // 2, 1)

    def set_modulation(s, f):
        log_sigma = jnp.log(sig[f, pl.ds(s, 1), :])
        smsh[f, 0] = 0.5 * (1.0 + log_sigma * mods[0])
        smsh[f, 1] = 0.5 * (log_sigma * mods[1])

    def send_far_pool(s):
        qsend[s] = (rate[1] * psend[s, 0] + psend[s, 1]).astype(WIRE)
        for d in range(1, n_chip):
            for to in range(2):

                @pl.when(chip + d < n_chip)
                def _():
                    far_pool_copy(s, d, to).start()

    for load in loads[0:3]:
        load.wait()
    sub = lax.broadcasted_iota(jnp.int32, (sig.shape[1], lon), 0)
    levels = jnp.ones((sig.shape[1], lon), F32)
    for s in range(STEPS + 1):
        levels = jnp.where(sub == s, plan[jnp.maximum(lvl[0] - s, 0)], levels)
    sig[core] = levels
    scale = in_scale_of(levels[0:1, :])
    for side, row in enumerate((0, rows - 1)):
        edge_row = win[pl.ds(row, chans, stride=rows), :]
        hsend[0, side, core, 0:chans, :] = (edge_row * scale).astype(BF16)
    for row in range(rows):
        home[row] = win[pl.ds(row, chans, stride=rows), :]
    for g in range(2):
        for r in range(2):
            csend[g, r] = home[their_row(g, r)]
            cur[core, g, r] = home[my_row(g, r)]
    for load in loads[3:7]:
        load.wait()
    mods[0] = jnp.broadcast_to(column(msc[...], 0, hidden), (hidden, lon))
    mods[1] = jnp.broadcast_to(column(msh[...], 0, hidden), (hidden, lon))
    eye = (
        lax.broadcasted_iota(jnp.int32, (chans, chans), 0)
        == lax.broadcasted_iota(jnp.int32, (chans, chans), 1)
    ).astype(F32).astype(BF16)
    liftw[...] = lax.dot_general(
        liftt[...], eye, (((0,), (0,)), ((), ())), preferred_element_type=F32
    ).astype(BF16)
    pl.semaphore_wait(barrier, n_hor - 1 + n_near * (1 + core))
    for side in range(2):

        @pl.when(has(side))
        def _():
            first_halo(side, core).start()

    sig_copy.start()
    ret_copy.start()
    cur_copy.start()
    for d in range(1, n_chip - 1):
        for to in range(2):

            @pl.when((chip >= 1) & (chip + d < n_chip))
            def _():
                far_rate_copy(d, to, core).start()

    set_modulation(0, core)
    for p in range(rows // 2):
        scaled = jnp.concatenate(
            [(home[2 * p + i] * scale).astype(BF16) for i in range(2)], axis=1
        )
        lifted = dot(liftw[...], scaled)
        for i in range(2):
            h = lifted[:, i * lon : (i + 1) * lon] * smsh[core, 0] + smsh[core, 1]
            feats0[2 * p + i] = half_silu(h).astype(BF16)
    for g in range(2):
        for r in range(2):
            xsend[2 * g + r] = feats0[their_row(g, r)]
        xsend[4 + g] = feats0[jnp.where(outer, 1 + g * (rows - 3), 2 + g * (rows - 5))]
    x_copy.start()
    pooled = jnp.zeros((hidden, lon), F32)
    for first in (0, 2):
        flat = [feats0[first + 4 * g + r] for g in range(2) for r in range(2)]
        pooled = pooled + dot(jnp.concatenate(flat, axis=1), poolm[...])
    psend[0, core] = packed(pooled)
    psend[0, other] = jnp.zeros((half, lon), F32)
    pool_copy(0).start()
    rate[core] = packed_rate(rets[core])
    for g in range(2):
        for r in range(2):
            place(feats0[my_row(g, r)].astype(F32), core, g, r)
        frecv[0, g, core] = feats0[jnp.where(outer, 2 + g * (rows - 5), 1 + g * (rows - 3))]
    remote(rets.at[other], rets.at[other], g_sem.at[2], g_sem.at[3], partner).wait_recv()
    rate[other] = packed_rate(rets[other])
    send_far_pool(0)
    remote(sig.at[other], sig.at[other], g_sem.at[0], g_sem.at[1], partner).wait_recv()
    set_modulation(0, other)
    for load in loads[7:]:
        load.wait()
    taps[...] = jnp.concatenate([convw[a] for a in range(3)], axis=1)
    x_copy.wait_recv()
    for g in range(2):
        for r in range(2):
            place(xrecv[2 * g + r].astype(F32), other, g, r)
        frecv[0, g, other] = xrecv[4 + g]
    remote(csend, cur.at[other], c_sem.at[0], c_sem.at[1], partner).wait_recv()
    for d in range(1, n_chip - 1):

        @pl.when(chip > d)
        def _():
            for c in range(2):
                far_rate_copy(d, 0, c).wait_recv()
            pair = packed_rate(rfar[d - 1, 0]) * packed_rate(rfar[d - 1, 1])
            coef[d] = pair if d == 1 else coef[d - 1] * pair

    @pl.loop(0, STEPS)
    def _(s):
        final = s == STEPS - 1
        keep, gain, scale_next = [], [], []
        for f in range(2):
            now, after = sig[f, pl.ds(s, 1), :], sig[f, pl.ds(s + 1, 1), :]
            ratio = after / now
            keep.append(ratio + (1.0 - ratio) / (now * now + 1.0))
            gain.append((1.0 - ratio) * (now * in_scale_of(now)))
            scale_next.append(in_scale_of(after))

        @pl.when(final & (chip > 0))
        def _():
            for g in range(2):
                for r in range(2):
                    base_send[g, r, 0:chans, :] = (keep[0] * cur[0, g, r]).astype(BF16)
            base_copy(core).start()

        for f in range(2):
            for g in range(2):
                wide = [
                    jnp.concatenate([stack[f, g, a], stack[f, g, a + 1]], axis=1)
                    for a in range(3)
                ]
                total = dot(taps[...], jnp.concatenate(wide, axis=0))
                for r in range(2):
                    acc[f, g, r] = total[:, r * lon : (r + 1) * lon]

        @pl.when(s > 0)
        def _():
            feat_copy(s).wait_recv()

        for g in range(2):
            rhs = [shifted(frecv[s, g, f].astype(F32)) for f in range(2)]
            extra = dot(convw[2 * joint(g)], jnp.concatenate(rhs, axis=1))
            for f in range(2):
                acc[f, g, joint(g)] += extra[:, f * lon : (f + 1) * lon]

        def remote_edges():
            for side in range(2):

                @pl.when(has(side) & (s == 0))
                def _():
                    for f in range(2):
                        first_halo(1 - side, f).wait_recv()

                @pl.when(has(side) & (s > 0))
                def _():
                    halo_copy(s, 1 - side).wait_recv()

            near = [hrecv[s, side, f, 0:chans, :] for side in range(2) for f in range(2)]
            near = dot(liftw[...], jnp.concatenate(near, axis=1))
            for side in range(2):
                rhs = []
                for f in range(2):
                    at = (2 * side + f) * lon
                    h = near[:, at : at + lon] * smsh[f, 0] + smsh[f, 1]
                    rhs.append(shifted(jnp.where(has(side), half_silu(h), 0.0)))
                extra = dot(convw[2 * side], jnp.concatenate(rhs, axis=1))
                for f in range(2):
                    acc[f, side, side] += extra[:, f * lon : (f + 1) * lon]

        def contexts():
            far[...] = jnp.zeros_like(far)
            for d in range(1, n_chip):

                @pl.when(chip >= d)
                def _():
                    for c in range(2):
                        far_pool_wait(s, d, c).wait_recv()
                    got = qrecv[s, d - 1, 0].astype(F32) + qrecv[s, d - 1, 1].astype(F32)
                    far[...] += got if d == 1 else coef[d - 1] * got

            pool_copy(s).wait_recv()
            first = rate[0] * far[...] + (psend[s, 0] + precv[s, 0])
            second = rate[1] * first + (psend[s, 1] + precv[s, 1])
            both = []
            for total in (first, second):
                high = total.astype(BF16)
                both.append(jnp.concatenate([high, (total - high.astype(F32)).astype(BF16)], axis=1))
            both = jnp.concatenate(both, axis=0)
            for side in range(2):
                wide = dot(both, spread[side])
                for f in range(2):
                    for tok in range(2):
                        up[f, tok, side * half : (side + 1) * half, :] = wide[
                            f * half : (f + 1) * half, tok * lon : (tok + 1) * lon
                        ]

        def finish(stage):
            cells = [(f, g, g if stage else 1 - g) for g in range(2) for f in range(2)]
            gated = []
            for f, g, r in cells:
                feat = stack[f, g, 1 + r, low].astype(F32)
                gated.append(half_silu(0.5 * (feat + acc[f, g, r] + up[f, g])).astype(BF16))
            outputs = dot(outw[...], jnp.concatenate(gated, axis=1))
            for i, (f, g, r) in enumerate(cells):
                nxt = keep[f] * cur[f, g, r] + gain[f] * outputs[:, i * lon : (i + 1) * lon]
                cur[f, g, r] = nxt
                if stage:
                    hsend[s + 1, g, f, 0:chans, :] = (nxt * scale_next[f]).astype(BF16)
                if f == 0:
                    rest_send[stage, g, 0:chans, :] = (
                        nxt - base_send[g, r, 0:chans, :].astype(F32)
                    ).astype(BF16)

            if stage:
                for side in range(2):

                    @pl.when(jnp.logical_not(final) & outer & has(side))
                    def _():
                        halo_copy(s + 1, side).start()

            @pl.when(final & (chip > 0))
            def _():
                rest_copy(stage, core).start()

        contexts()
        finish(0)

        @pl.when(outer)
        def _():
            remote_edges()

        finish(1)

        @pl.when(jnp.logical_not(final))
        def _():
            for f in range(2):
                set_modulation(s + 1, f)
            for f in range(2):
                for g in range(2):
                    scaled = jnp.concatenate(
                        [(cur[f, g, r] * scale_next[f]).astype(BF16) for r in range(2)], axis=1
                    )
                    lifted = dot(liftw[...], scaled)
                    for r in range(2):
                        h = lifted[:, r * lon : (r + 1) * lon] * smsh[f, 0] + smsh[f, 1]
                        place(half_silu(h), f, g, r)
            for g in range(2):
                for f in range(2):
                    fsend[s + 1, g, f] = stack[f, g, 1 + joint(g), low]
            feat_copy(s + 1).start()
            flat = [
                jnp.concatenate([stack[f, g, 1 + r, low] for g in range(2) for r in range(2)], axis=1)
                for f in range(2)
            ]
            pooled = dot(jnp.concatenate(flat, axis=0), poolm[...])
            for f in range(2):
                psend[s + 1, f] = packed(pooled[f * hidden : (f + 1) * hidden])
            pool_copy(s + 1).start()
            send_far_pool(s + 1)

    final_copy(1).start()

    @pl.when(outer)
    def _():
        final_copy(0).start()

    def put(out, row, value):
        out[pl.ds(row, chans, stride=rows), :] = value

    cells = [(g, r) for g in range(2) for r in range(2)]

    @pl.when(outer)
    def _():
        for g, r in cells:
            put(wout, outer_row(g, r), cur[1, g, r])

        final_copy(1).wait_recv()
        for g, r in cells:
            put(wout, inner_row(g, r), fin_recv[1, g, r])

        @pl.when(chip == n_chip - 1)
        def _():
            fresh_load.wait()
            arr[...] = plan[plan.shape[0] - 1] * arr[...]

        @pl.when(chip < n_chip - 1)
        def _():
            for c in range(2):
                base_copy(c).wait_recv()
            for stage in range(2):
                for c in range(2):
                    rest_copy(stage, c).wait_recv()
                    for g in range(2):
                        r = g if stage else 1 - g
                        row = outer_row(g, r) if c else inner_row(g, r)
                        value = base_recv[c, g, r, 0:chans, :].astype(F32)
                        put(arr, row, value + rest_recv[c, stage, g, 0:chans, :].astype(F32))

    @pl.when(jnp.logical_not(outer))
    def _():
        for g, r in cells:
            put(wout, inner_row(g, r), cur[0, g, r])
            put(arr, inner_row(g, r), cur[1, g, r])
        for f, out in ((1, arr), (0, wout)):
            final_copy(f).wait_recv()
            for g, r in cells:
                put(out, outer_row(g, r), fin_recv[f, g, r])

    for copy in (sig_copy, ret_copy, cur_copy, x_copy, final_copy(1)):
        copy.wait_send()
    for side in range(2):

        @pl.when(has(side))
        def _():
            first_halo(side, core).wait_send()

    for d in range(1, n_chip):
        for to in range(2):

            @pl.when(chip + d < n_chip)
            def _():
                for s in range(STEPS):
                    far_pool_copy(s, d, to).wait_send()

    for d in range(1, n_chip - 1):
        for to in range(2):

            @pl.when((chip >= 1) & (chip + d < n_chip))
            def _():
                far_rate_copy(d, to, core).wait_send()

    for s in range(STEPS):
        pool_copy(s).wait_send()
        if s:
            feat_copy(s).wait_send()
            for side in range(2):

                @pl.when(outer & has(side))
                def _():
                    halo_copy(s, side).wait_send()

    @pl.when(outer)
    def _():
        final_copy(0).wait_send()

    @pl.when(chip > 0)
    def _():
        base_copy(core).wait_send()
        for stage in range(2):
            rest_copy(stage, core).wait_send()


def write(a, b, a_out, b_out, sem):
    copies = [pltpu.make_async_copy(x, y, sem.at[i]) for i, (x, y) in enumerate([(a, a_out), (b, b_out)])]
    for copy in copies:
        copy.start()
    for copy in copies:
        copy.wait()


def body(
    n_hor,
    n_lat,
    window,
    fresh_noise,
    level_index,
    plan,
    retention,
    lift_weight,
    mod_scale,
    mod_shift,
    conv_weight,
    out_weight,
):
    frames, chans, rows, lon = window.shape
    hidden = conv_weight.shape[1]
    half = hidden // 2
    cpad = -(-chans // 16) * 16
    n_chip = n_hor // 2
    peers = max(1, n_chip - 1)
    vmem = pl.BlockSpec(memory_space=pltpu.VMEM)
    hbm = pl.BlockSpec(memory_space=pltpu.HBM)
    flat = jax.ShapeDtypeStruct((chans * rows, lon), F32)
    dma = pltpu.SemaphoreType.DMA
    current, arriving = pl.pallas_call(
        functools.partial(kernel, rows, lon, n_hor, n_lat),
        out_shape=(pltpu.VMEM(flat.shape, F32), pltpu.VMEM(flat.shape, F32)),
        in_specs=[hbm] * 10,
        out_specs=(vmem, vmem),
        scratch_shapes=[
            pltpu.SMEM(level_index.shape, jnp.int32),
            pltpu.SMEM(plan.shape, F32),
            pltpu.VMEM((chans * rows, lon), F32),
            pltpu.VMEM((2, 1, hidden), F32),
            pltpu.VMEM((peers, 2, 1, hidden), F32),
            pltpu.VMEM((1, hidden), F32),
            pltpu.VMEM((1, hidden), F32),
            pltpu.VMEM((chans, hidden), BF16),
            pltpu.VMEM(conv_weight.shape, BF16),
            pltpu.VMEM((chans, hidden), BF16),
            pltpu.VMEM((hidden, chans), BF16),
            pltpu.VMEM((hidden, 9 * hidden), BF16),
            pltpu.VMEM((rows, chans, lon), F32),
            pltpu.VMEM((rows, hidden, lon), BF16),
            pltpu.VMEM((2, 2, chans, lon), F32),
            pltpu.VMEM((6, hidden, lon), BF16),
            pltpu.VMEM((6, hidden, lon), BF16),
            pltpu.VMEM((2, 2, 2, chans, lon), F32),
            pltpu.VMEM((2, 2, 5, 3 * hidden, lon), BF16),
            pltpu.VMEM((STEPS, 2, 2, hidden, lon), BF16),
            pltpu.VMEM((STEPS, 2, 2, hidden, lon), BF16),
            pltpu.VMEM((2, 2, 2, hidden, lon), F32),
            pltpu.VMEM((2, 2, hidden, lon), F32),
            pltpu.VMEM((2, hidden, lon), F32),
            pltpu.VMEM((2, 2, hidden, lon), F32),
            pltpu.VMEM((2, 8, lon), F32),
            pltpu.VMEM((4 * lon, lon), BF16),
            pltpu.VMEM((2, 2 * lon, 2 * lon), BF16),
            pltpu.VMEM((2, half, lon), F32),
            pltpu.VMEM((peers, half, lon), F32),
            pltpu.VMEM((half, lon), F32),
            pltpu.VMEM((STEPS + 1, 2, 2, cpad, lon), BF16),
            pltpu.VMEM((STEPS, 2, 2, cpad, lon), BF16),
            pltpu.VMEM((STEPS, 2, half, lon), F32),
            pltpu.VMEM((STEPS, 2, half, lon), F32),
            pltpu.VMEM((STEPS, half, lon), WIRE),
            pltpu.VMEM((STEPS, peers, 2, half, lon), WIRE),
            pltpu.VMEM((2, 2, cpad, lon), BF16),
            pltpu.VMEM((2, 2, 2, cpad, lon), BF16),
            pltpu.VMEM((2, 2, cpad, lon), BF16),
            pltpu.VMEM((2, 2, 2, cpad, lon), BF16),
            pltpu.VMEM((2, 2, 2, chans, lon), F32),
            dma((10,)),
            dma((4,)),
            dma((4,)),
            dma((2, STEPS, 2)),
            dma((2, 2, 2)),
            dma((2, STEPS)),
            dma((2, STEPS)),
            dma((STEPS, peers, 2)),
            dma((STEPS, peers, 2)),
            dma((peers, 2)),
            dma((peers, 2)),
            dma((3,)),
            dma((3, 2)),
            dma((2, 2)),
        ],
        compiler_params=pltpu.CompilerParams(
            collective_id=0, has_side_effects=True, vmem_limit_bytes=66400000
        ),
    )(
        level_index,
        plan,
        window.reshape(chans * rows, lon),
        fresh_noise.reshape(chans * rows, lon),
        retention,
        mod_scale.reshape(1, hidden),
        mod_shift.reshape(1, hidden),
        lift_weight.T,
        conv_weight,
        out_weight,
    )
    shape = (frames, chans, rows, lon)
    current, rolled = pl.pallas_call(
        write,
        out_shape=(flat, flat),
        in_specs=[vmem, vmem],
        out_specs=(hbm, hbm),
        scratch_shapes=[dma((2,))],
        compiler_params=pltpu.CompilerParams(vmem_limit_bytes=4 * 1024 * 1024),
    )(current, arriving)
    return (current.reshape(shape), rolled.reshape(shape))


def solution(mesh):
    in_specs = (
        P("hor", None, "lat", None),
        P(None, "lat", None),
        P("hor"),
        P(),
        P("hor", None),
        P(),
        P(),
        P(),
        P(),
        P(),
    )
    out_specs = (P("hor", None, "lat", None), P("hor", None, "lat", None))
    run = functools.partial(body, mesh.shape["hor"], mesh.shape["lat"])
    return jax.shard_map(run, mesh=mesh, in_specs=in_specs, out_specs=out_specs, check_vma=False)
```

time: 21.3 us -> 21.4 us (level)
  no operation moved by 1% of the time
where the time goes in v2:
time: 21.4 us; the launch traced here: 21.2 us
  Pallas kernels  19.9 us (93%)
  between operations  1.29 us (6%)
    pallas_call x1, Pallas kernels, body(): pl.pallas_call(functools.partial(kernel, rows, lon, n_hor, n_lat), out_sh...  19.1 us
    pallas_call x1, Pallas kernels, body(): pl.pallas_call(write, out_shape=(flat, flat), in_specs=[vmem, vmem], out_...  0.82 us

profile of v2, /device:TPU:1, one launch (start us, length us, event | category | flops | bytes accessed | tf_op | source)
XLA Modules:
  0.0 21.2 jit_solution(13728429141732061432)
XLA Ops:
  1.3 19.1 %shard_map.113 = (f32[552,128]{1,0:T(8,128)S(1)}, f32[552,128]{1,0:T(8,128)S(1)}) custom-call(s32[1]{0:T(128)S(6)} %copy.12.lvl_h, f32[64]{0:T(128)} %plan_h.1, f32[552,128]{1,0:T(8,128)} %bitcast.7, f32[552,128]{1,0:T(8,128)} %bitcast.8, f32[1,192]{1,0:T(1,128)} %ret_h.1, f32[1,192]{1,0:T(1,128)} %bitcast.10, f32[1,192]{1,0:T(1,128)} %bitcast.11, ...), custom_call_target="tpu_custom_call" | custom-call | tf_op jit(solution)/shard_map/pallas_call | solution.py:685
  20.4 0.8 %shard_map.114 = (f32[552,128]{1,0:T(8,128)}, f32[552,128]{1,0:T(8,128)}) custom-call(f32[552,128]{1,0:T(8,128)S(1)} %get-tuple-element.6.a, f32[552,128]{1,0:T(8,128)S(1)} %get-tuple-element.7.b), custom_call_target="tpu_custom_call" | custom-call | tf_op jit(solution)/shard_map/pallas_call | solution.py:764

commit v3 on v2

--- a/solution.py
+++ b/solution.py
@@ -54,10 +54,12 @@
     xsend,
     xrecv,
     cur,
-    stack,
+    stack_a,
+    stack_b,
     fsend,
     frecv,
-    acc,
+    acc_a,
+    acc_b,
     up,
     mods,
     smsh,
@@ -66,7 +68,7 @@
     spread,
     rate,
     coef,
-    far,
+    raw_rate,
     hsend,
     hrecv,
     psend,
@@ -82,7 +84,6 @@
     c_sem,
     g_sem,
     h_sem,
-    h0_sem,
     f_sem,
     p_sem,
     q_ssem,
@@ -96,6 +97,7 @@
     hidden, chans = liftw.shape
     half = hidden // 2
     n_chip = n_hor // 2
+    stack, acc = (stack_a, stack_b), (acc_a, acc_b)
     hor = lax.axis_index("hor")
     lat = lax.axis_index("lat")
     chip = hor // 2
@@ -156,9 +158,8 @@
             hrecv[:, side] = jnp.zeros_like(hrecv[:, side])
 
     for f in range(2):
-        for g in range(2):
-            for block in (0, 3):
-                stack[f, g, block] = jnp.zeros_like(stack[f, g, block])
+        for block in (0, 5):
+            stack[f][block] = jnp.zeros_like(stack[f][block])
 
     def column(row_ref_value, start, count):
         sub = lax.broadcasted_iota(jnp.int32, (count, hidden), 0) + start
@@ -200,30 +201,21 @@
     def their_row(g, r):
         return jnp.where(outer, inner_row(g, r), outer_row(g, r))
 
-    def joint(g):
-        return jnp.where(outer, 1 - g, g)
+    def joint(g, c):
+        return 1 - g if c else g
 
     sig_copy = remote(sig.at[core], sig.at[core], g_sem.at[0], g_sem.at[1], partner)
     ret_copy = remote(rets.at[core], rets.at[core], g_sem.at[2], g_sem.at[3], partner)
     cur_copy = remote(csend, cur.at[core], c_sem.at[0], c_sem.at[1], partner)
     x_copy = remote(xsend, xrecv, c_sem.at[2], c_sem.at[3], partner)
 
-    def first_halo(side, f):
+    def halo_copy(s, side, f):
         return remote(
-            hsend.at[0, side, f],
-            hrecv.at[0, 1 - side, f],
-            h0_sem.at[0, side, f],
-            h0_sem.at[1, 1 - side, f],
+            hsend.at[s, side, f],
+            hrecv.at[s, 1 - side, f],
+            h_sem.at[0, s, side, f],
+            h_sem.at[1, s, 1 - side, f],
             {"hor": 2 * chip + 1, "lat": lat - 1 + 2 * side},
-        )
-
-    def halo_copy(s, side):
-        return remote(
-            hsend.at[s, side],
-            hrecv.at[s, 1 - side],
-            h_sem.at[0, s, side],
-            h_sem.at[1, s, 1 - side],
-            {"lat": lat - 1 + 2 * side},
         )
 
     def feat_copy(s):
@@ -287,23 +279,36 @@
     low = slice(hidden, 2 * hidden)
 
     def place(feat, f, g, r):
-        parts = shifted(feat)
-        stack[f, g, 1 + r] = parts
-        if (g, r) == (0, 1):
-            stack[f, 1, jnp.where(outer, 4, 0)] = parts
-        if (g, r) == (1, 0):
-            stack[f, 0, jnp.where(outer, 4, 3)] = parts
+        stack[f][1 + 2 * g + r] = shifted(feat)
+
+    def feature(f, g, r):
+        return stack[f][1 + 2 * g + r, low]
+
+    def convolve(f, c, s):
+        for g in range(2):
+            blocks = [0, 1, 2, 6 if c else 3] if g == 0 else [7 if c else 2, 3, 4, 5]
+            if c:
+                stack[f][6 + g] = shifted(frecv[s, g, f].astype(F32))
+            wide = [
+                jnp.concatenate([stack[f][blocks[a]], stack[f][blocks[a + 1]]], axis=1)
+                for a in range(3)
+            ]
+            total = dot(taps[...], jnp.concatenate(wide, axis=0))
+            for r in range(2):
+                acc[f][g, r] = total[:, r * lon : (r + 1) * lon]
 
     def packed(value):
         return value[0:half] + pltpu.roll(value[half:hidden], lon // 2, 1)
 
     def set_modulation(s, f):
         log_sigma = jnp.log(sig[f, pl.ds(s, 1), :])
-        smsh[f, 0] = 0.5 * (1.0 + log_sigma * mods[0])
-        smsh[f, 1] = 0.5 * (log_sigma * mods[1])
+        smsh[lax.rem(s, 2), f, 0] = 0.5 * (1.0 + log_sigma * mods[0])
+        smsh[lax.rem(s, 2), f, 1] = 0.5 * (log_sigma * mods[1])
+
+    def modulate(value, s, f):
+        return half_silu(value * smsh[lax.rem(s, 2), f, 0] + smsh[lax.rem(s, 2), f, 1])
 
     def send_far_pool(s):
-        qsend[s] = (rate[1] * psend[s, 0] + psend[s, 1]).astype(WIRE)
         for d in range(1, n_chip):
             for to in range(2):
 
@@ -328,6 +333,9 @@
         for r in range(2):
             csend[g, r] = home[their_row(g, r)]
             cur[core, g, r] = home[my_row(g, r)]
+            xsend[2 * g + r] = (csend[g, r] * scale).astype(BF16)
+        joint_row = jnp.where(outer, 1 + g * (rows - 3), 2 + g * (rows - 5))
+        xsend[4 + g] = (home[joint_row] * scale).astype(BF16)
     for load in loads[3:7]:
         load.wait()
     mods[0] = jnp.broadcast_to(column(msc[...], 0, hidden), (hidden, lon))
@@ -339,23 +347,6 @@
     liftw[...] = lax.dot_general(
         liftt[...], eye, (((0,), (0,)), ((), ())), preferred_element_type=F32
     ).astype(BF16)
-    pl.semaphore_wait(barrier, n_hor - 1 + n_near * (1 + core))
-    for side in range(2):
-
-        @pl.when(has(side))
-        def _():
-            first_halo(side, core).start()
-
-    sig_copy.start()
-    ret_copy.start()
-    cur_copy.start()
-    for d in range(1, n_chip - 1):
-        for to in range(2):
-
-            @pl.when((chip >= 1) & (chip + d < n_chip))
-            def _():
-                far_rate_copy(d, to, core).start()
-
     set_modulation(0, core)
     for p in range(rows // 2):
         scaled = jnp.concatenate(
@@ -363,51 +354,83 @@
         )
         lifted = dot(liftw[...], scaled)
         for i in range(2):
-            h = lifted[:, i * lon : (i + 1) * lon] * smsh[core, 0] + smsh[core, 1]
-            feats0[2 * p + i] = half_silu(h).astype(BF16)
-    for g in range(2):
-        for r in range(2):
-            xsend[2 * g + r] = feats0[their_row(g, r)]
-        xsend[4 + g] = feats0[jnp.where(outer, 1 + g * (rows - 3), 2 + g * (rows - 5))]
+            feats0[2 * p + i] = modulate(lifted[:, i * lon : (i + 1) * lon], 0, core).astype(BF16)
+    pl.semaphore_wait(barrier, n_hor - 1 + n_near * (1 + core))
+    even = lax.rem(lat, 2) == 0
+    send_order = [(0, even), (1, lat >= 0), (0, jnp.logical_not(even))]
+    for side, when in send_order:
+
+        @pl.when(has(side) & when)
+        def _():
+            halo_copy(0, side, core).start()
+
+    sig_copy.start()
     x_copy.start()
+    ret_copy.start()
+    cur_copy.start()
     pooled = jnp.zeros((hidden, lon), F32)
     for first in (0, 2):
         flat = [feats0[first + 4 * g + r] for g in range(2) for r in range(2)]
         pooled = pooled + dot(jnp.concatenate(flat, axis=1), poolm[...])
-    psend[0, core] = packed(pooled)
+    pooled = packed(pooled)
+    qsend[0] = pooled.astype(WIRE)
+    psend[0, core] = pooled
     psend[0, other] = jnp.zeros((half, lon), F32)
+    send_far_pool(0)
     pool_copy(0).start()
     rate[core] = packed_rate(rets[core])
-    for g in range(2):
-        for r in range(2):
-            place(feats0[my_row(g, r)].astype(F32), core, g, r)
-        frecv[0, g, core] = feats0[jnp.where(outer, 2 + g * (rows - 5), 1 + g * (rows - 3))]
-    remote(rets.at[other], rets.at[other], g_sem.at[2], g_sem.at[3], partner).wait_recv()
-    rate[other] = packed_rate(rets[other])
-    send_far_pool(0)
-    remote(sig.at[other], sig.at[other], g_sem.at[0], g_sem.at[1], partner).wait_recv()
-    set_modulation(0, other)
+    for d in range(1, n_chip):
+        for to in range(2):
+
+            @pl.when(chip + d < n_chip)
+            def _():
+                far_rate_copy(d, to, core).start()
+
     for load in loads[7:]:
         load.wait()
     taps[...] = jnp.concatenate([convw[a] for a in range(3)], axis=1)
-    x_copy.wait_recv()
-    for g in range(2):
-        for r in range(2):
-            place(xrecv[2 * g + r].astype(F32), other, g, r)
-        frecv[0, g, other] = xrecv[4 + g]
+
+    for c in range(2):
+
+        @pl.when(core == c)
+        def _():
+            row_of = outer_row if c else inner_row
+            for g in range(2):
+                for r in range(2):
+                    place(feats0[row_of(g, r)].astype(F32), c, g, r)
+                frecv[0, g, c] = feats0[(2 + g * (rows - 5)) if c else (1 + g * (rows - 3))]
+            convolve(c, c, 0)
+            remote(sig.at[1 - c], sig.at[1 - c], g_sem.at[0], g_sem.at[1], partner).wait_recv()
+            set_modulation(0, 1 - c)
+            x_copy.wait_recv()
+            for p in range(3):
+                got = jnp.concatenate([xrecv[2 * p], xrecv[2 * p + 1]], axis=1)
+                lifted = dot(liftw[...], got)
+                for i in range(2):
+                    feat = modulate(lifted[:, i * lon : (i + 1) * lon], 0, 1 - c)
+                    if p < 2:
+                        place(feat, 1 - c, p, i)
+                    else:
+                        frecv[0, i, 1 - c] = feat.astype(BF16)
+            convolve(1 - c, c, 0)
+
+    remote(rets.at[other], rets.at[other], g_sem.at[2], g_sem.at[3], partner).wait_recv()
+    rate[other] = packed_rate(rets[other])
     remote(csend, cur.at[other], c_sem.at[0], c_sem.at[1], partner).wait_recv()
-    for d in range(1, n_chip - 1):
-
-        @pl.when(chip > d)
-        def _():
-            for c in range(2):
-                far_rate_copy(d, 0, c).wait_recv()
-            pair = packed_rate(rfar[d - 1, 0]) * packed_rate(rfar[d - 1, 1])
-            coef[d] = pair if d == 1 else coef[d - 1] * pair
-
-    @pl.loop(0, STEPS)
-    def _(s):
-        final = s == STEPS - 1
+    def far_rates():
+        for d in range(1, n_chip):
+
+            @pl.when(chip >= d)
+            def _():
+                for c in range(2):
+                    far_rate_copy(d, 0, c).wait_recv()
+                second = packed_rate(rfar[d - 1, 1])
+                raw_rate[d - 1] = second
+                if d < n_chip - 1:
+                    pair = packed_rate(rfar[d - 1, 0]) * second
+                    coef[d] = pair if d == 1 else coef[d - 1] * pair
+
+    def step(s, final):
         keep, gain, scale_next = [], [], []
         for f in range(2):
             now, after = sig[f, pl.ds(s, 1), :], sig[f, pl.ds(s + 1, 1), :]
@@ -416,70 +439,77 @@
             gain.append((1.0 - ratio) * (now * in_scale_of(now)))
             scale_next.append(in_scale_of(after))
 
-        @pl.when(final & (chip > 0))
-        def _():
+        if not final:
+
+            @pl.when((s == STEPS - 2) & (chip > 0))
+            def _():
+                last, end = sig[0, pl.ds(s + 1, 1), :], sig[0, pl.ds(s + 2, 1), :]
+                hold = keep[0] * (end / last + (1.0 - end / last) / (last * last + 1.0))
+                for g in range(2):
+                    for r in range(2):
+                        base_send[g, r, 0:chans, :] = (hold * cur[0, g, r]).astype(BF16)
+                base_copy(core).start()
+
+        def await_feats():
+            @pl.when(s > 0)
+            def _():
+                feat_copy(s).wait_recv()
+
+        def joint_edges(c):
             for g in range(2):
-                for r in range(2):
-                    base_send[g, r, 0:chans, :] = (keep[0] * cur[0, g, r]).astype(BF16)
-            base_copy(core).start()
-
-        for f in range(2):
-            for g in range(2):
-                wide = [
-                    jnp.concatenate([stack[f, g, a], stack[f, g, a + 1]], axis=1)
-                    for a in range(3)
-                ]
-                total = dot(taps[...], jnp.concatenate(wide, axis=0))
-                for r in range(2):
-                    acc[f, g, r] = total[:, r * lon : (r + 1) * lon]
-
-        @pl.when(s > 0)
-        def _():
-            feat_copy(s).wait_recv()
-
-        for g in range(2):
-            rhs = [shifted(frecv[s, g, f].astype(F32)) for f in range(2)]
-            extra = dot(convw[2 * joint(g)], jnp.concatenate(rhs, axis=1))
-            for f in range(2):
-                acc[f, g, joint(g)] += extra[:, f * lon : (f + 1) * lon]
-
-        def remote_edges():
+                j = joint(g, c)
+                rhs = [shifted(frecv[s, g, f].astype(F32)) for f in range(2)]
+                extra = dot(convw[2 * j], jnp.concatenate(rhs, axis=1))
+                for f in range(2):
+                    acc[f][g, j] += extra[:, f * lon : (f + 1) * lon]
+
+        def await_halos(f):
             for side in range(2):
 
-                @pl.when(has(side) & (s == 0))
+                @pl.when(has(side))
                 def _():
-                    for f in range(2):
-                        first_halo(1 - side, f).wait_recv()
-
-                @pl.when(has(side) & (s > 0))
-                def _():
-                    halo_copy(s, 1 - side).wait_recv()
-
-            near = [hrecv[s, side, f, 0:chans, :] for side in range(2) for f in range(2)]
+                    halo_copy(s, 1 - side, f).wait_recv()
+
+        def remote_edges(frames):
+            near = [hrecv[s, side, f, 0:chans, :] for side in range(2) for f in frames]
             near = dot(liftw[...], jnp.concatenate(near, axis=1))
             for side in range(2):
                 rhs = []
-                for f in range(2):
-                    at = (2 * side + f) * lon
-                    h = near[:, at : at + lon] * smsh[f, 0] + smsh[f, 1]
-                    rhs.append(shifted(jnp.where(has(side), half_silu(h), 0.0)))
+                for i, f in enumerate(frames):
+                    at = (side * len(frames) + i) * lon
+                    feat = modulate(near[:, at : at + lon], s, f)
+                    rhs.append(shifted(jnp.where(has(side), feat, 0.0)))
                 extra = dot(convw[2 * side], jnp.concatenate(rhs, axis=1))
-                for f in range(2):
-                    acc[f, side, side] += extra[:, f * lon : (f + 1) * lon]
+                for i, f in enumerate(frames):
+                    acc[f][side, side] += extra[:, i * lon : (i + 1) * lon]
+
+        def await_pools():
+            if not final:
+
+                @pl.when(s == 0)
+                def _():
+                    far_rates()
+
+            pool_copy(s).wait_recv()
+            for d in range(1, n_chip):
+                for c in range(2):
+
+                    @pl.when(chip >= d)
+                    def _():
+                        far_pool_wait(s, d, c).wait_recv()
 
         def contexts():
-            far[...] = jnp.zeros_like(far)
-            for d in range(1, n_chip):
-
-                @pl.when(chip >= d)
-                def _():
-                    for c in range(2):
-                        far_pool_wait(s, d, c).wait_recv()
-                    got = qrecv[s, d - 1, 0].astype(F32) + qrecv[s, d - 1, 1].astype(F32)
-                    far[...] += got if d == 1 else coef[d - 1] * got
-
-            pool_copy(s).wait_recv()
-            first = rate[0] * far[...] + (psend[s, 0] + precv[s, 0])
+            first = psend[s, 0] + precv[s, 0]
+            if n_chip > 1:
+                total = jnp.zeros((half, lon), F32)
+                for d in range(1, n_chip):
+                    got = qrecv[s, d - 1, 0].astype(F32)
+                    if not final:
+                        got = got * jnp.where(s == 0, raw_rate[d - 1], 1.0)
+                    got = got + qrecv[s, d - 1, 1].astype(F32)
+                    got = got if d == 1 else coef[d - 1] * got
+                    total = total + jnp.where(chip >= d, got, 0.0)
+                first = first + rate[0] * total
             second = rate[1] * first + (psend[s, 1] + precv[s, 1])
             both = []
             for total in (first, second):
@@ -494,75 +524,128 @@
                             f * half : (f + 1) * half, tok * lon : (tok + 1) * lon
                         ]
 
-        def finish(stage):
-            cells = [(f, g, g if stage else 1 - g) for g in range(2) for f in range(2)]
+        def finish(cells):
             gated = []
             for f, g, r in cells:
-                feat = stack[f, g, 1 + r, low].astype(F32)
-                gated.append(half_silu(0.5 * (feat + acc[f, g, r] + up[f, g])).astype(BF16))
+                feat = feature(f, g, r).astype(F32)
+                gated.append(half_silu(0.5 * (feat + acc[f][g, r] + up[f, g])).astype(BF16))
             outputs = dot(outw[...], jnp.concatenate(gated, axis=1))
             for i, (f, g, r) in enumerate(cells):
                 nxt = keep[f] * cur[f, g, r] + gain[f] * outputs[:, i * lon : (i + 1) * lon]
                 cur[f, g, r] = nxt
-                if stage:
+                if g == r and not final:
                     hsend[s + 1, g, f, 0:chans, :] = (nxt * scale_next[f]).astype(BF16)
-                if f == 0:
-                    rest_send[stage, g, 0:chans, :] = (
+                if f == 0 and final:
+                    rest_send[1 if g == r else 0, g, 0:chans, :] = (
                         nxt - base_send[g, r, 0:chans, :].astype(F32)
                     ).astype(BF16)
 
-            if stage:
-                for side in range(2):
-
-                    @pl.when(jnp.logical_not(final) & outer & has(side))
-                    def _():
-                        halo_copy(s + 1, side).start()
-
-            @pl.when(final & (chip > 0))
+        def send_rest(stage):
+            @pl.when(chip > 0)
             def _():
                 rest_copy(stage, core).start()
 
-        contexts()
-        finish(0)
-
-        @pl.when(outer)
-        def _():
-            remote_edges()
-
-        finish(1)
-
-        @pl.when(jnp.logical_not(final))
-        def _():
-            for f in range(2):
-                set_modulation(s + 1, f)
+        def lift(pairs):
+            for pair in pairs:
+                f = pair[0][0]
+                scaled = jnp.concatenate(
+                    [(cur[cell] * scale_next[f]).astype(BF16) for cell in pair], axis=1
+                )
+                lifted = dot(liftw[...], scaled)
+                for i, cell in enumerate(pair):
+                    place(modulate(lifted[:, i * lon : (i + 1) * lon], s + 1, f), *cell)
+
+        def send_feats(c):
             for f in range(2):
                 for g in range(2):
-                    scaled = jnp.concatenate(
-                        [(cur[f, g, r] * scale_next[f]).astype(BF16) for r in range(2)], axis=1
-                    )
-                    lifted = dot(liftw[...], scaled)
-                    for r in range(2):
-                        h = lifted[:, r * lon : (r + 1) * lon] * smsh[f, 0] + smsh[f, 1]
-                        place(half_silu(h), f, g, r)
-            for g in range(2):
-                for f in range(2):
-                    fsend[s + 1, g, f] = stack[f, g, 1 + joint(g), low]
+                    fsend[s + 1, g, f] = feature(f, g, joint(g, c))
             feat_copy(s + 1).start()
+
+        def send_pools():
             flat = [
-                jnp.concatenate([stack[f, g, 1 + r, low] for g in range(2) for r in range(2)], axis=1)
+                jnp.concatenate([feature(f, g, r) for g in range(2) for r in range(2)], axis=1)
                 for f in range(2)
             ]
             pooled = dot(jnp.concatenate(flat, axis=0), poolm[...])
+            first, second = (packed(pooled[f * hidden : (f + 1) * hidden]) for f in range(2))
+            qsend[s + 1] = (rate[1] * first + second).astype(WIRE)
+            send_far_pool(s + 1)
+            psend[s + 1, 0] = first
+            psend[s + 1, 1] = second
+            pool_copy(s + 1).start()
+
+        near_cells = [[(f, 0, 1), (f, 1, 0)] for f in range(2)]
+        edge_cells = [[(f, 0, 0), (f, 1, 1)] for f in range(2)]
+
+        def send_edges():
+            for side, when in send_order:
+
+                @pl.when(has(side) & when)
+                def _():
+                    for f in range(2):
+                        halo_copy(s + 1, side, f).start()
+
+        all_near, all_edge = near_cells[0] + near_cells[1], edge_cells[0] + edge_cells[1]
+
+        @pl.when(outer)
+        def _():
+            await_pools()
+            contexts()
+            finish(all_near)
+            if final:
+                send_rest(0)
             for f in range(2):
-                psend[s + 1, f] = packed(pooled[f * hidden : (f + 1) * hidden])
-            pool_copy(s + 1).start()
-            send_far_pool(s + 1)
-
-    final_copy(1).start()
-
-    @pl.when(outer)
-    def _():
-        final_copy(0).start()
+                await_halos(f)
+            remote_edges([0, 1])
+            finish(all_edge)
+            if final:
+                send_rest(1)
+            else:
+                send_edges()
+
+            if final:
+                for f in range(2):
+                    final_copy(f).start()
+            else:
+                for f in range(2):
+                    set_modulation(s + 1, f)
+                lift(near_cells)
+                send_feats(1)
+                lift(edge_cells)
+                send_pools()
+                feat_copy(s + 1).wait_recv()
+                for f in range(2):
+                    convolve(f, 1, s + 1)
+
+        @pl.when(jnp.logical_not(outer))
+        def _():
+            await_feats()
+            joint_edges(0)
+            await_pools()
+            contexts()
+            if final:
+                finish(near_cells[0] + edge_cells[0])
+                send_rest(0)
+                send_rest(1)
+                finish(near_cells[1] + edge_cells[1])
+                final_copy(1).start()
+            else:
+                finish(near_cells[0] + edge_cells[0])
+                finish(near_cells[1] + edge_cells[1])
+                for f in range(2):
+                    set_modulation(s + 1, f)
+                lift(edge_cells)
+                send_feats(0)
+                lift(near_cells)
+                send_pools()
+                for f in range(2):
+                    convolve(f, 0, s + 1)
+
+    @pl.loop(0, STEPS - 1)
+    def _(s):
+        step(s, False)
+
+    step(STEPS - 1, True)
 
     def put(out, row, value):
         out[pl.ds(row, chans, stride=rows), :] = value
@@ -612,7 +695,7 @@
 
         @pl.when(has(side))
         def _():
-            first_halo(side, core).wait_send()
+            halo_copy(0, side, core).wait_send()
 
     for d in range(1, n_chip):
         for to in range(2):
@@ -622,10 +705,10 @@
                 for s in range(STEPS):
                     far_pool_copy(s, d, to).wait_send()
 
-    for d in range(1, n_chip - 1):
+    for d in range(1, n_chip):
         for to in range(2):
 
-            @pl.when((chip >= 1) & (chip + d < n_chip))
+            @pl.when(chip + d < n_chip)
             def _():
                 far_rate_copy(d, to, core).wait_send()
 
@@ -637,7 +720,8 @@
 
                 @pl.when(outer & has(side))
                 def _():
-                    halo_copy(s, side).wait_send()
+                    for f in range(2):
+                        halo_copy(s, side, f).wait_send()
 
     @pl.when(outer)
     def _():
@@ -675,7 +759,7 @@
     frames, chans, rows, lon = window.shape
     hidden = conv_weight.shape[1]
     half = hidden // 2
-    cpad = -(-chans // 16) * 16
+    cpad = -(-chans // 8) * 8
     n_chip = n_hor // 2
     peers = max(1, n_chip - 1)
     vmem = pl.BlockSpec(memory_space=pltpu.VMEM)
@@ -703,22 +787,24 @@
             pltpu.VMEM((rows, chans, lon), F32),
             pltpu.VMEM((rows, hidden, lon), BF16),
             pltpu.VMEM((2, 2, chans, lon), F32),
-            pltpu.VMEM((6, hidden, lon), BF16),
-            pltpu.VMEM((6, hidden, lon), BF16),
+            pltpu.VMEM((6, chans, lon), BF16),
+            pltpu.VMEM((6, chans, lon), BF16),
             pltpu.VMEM((2, 2, 2, chans, lon), F32),
-            pltpu.VMEM((2, 2, 5, 3 * hidden, lon), BF16),
+            pltpu.VMEM((8, 3 * hidden, lon), BF16),
+            pltpu.VMEM((8, 3 * hidden, lon), BF16),
             pltpu.VMEM((STEPS, 2, 2, hidden, lon), BF16),
             pltpu.VMEM((STEPS, 2, 2, hidden, lon), BF16),
-            pltpu.VMEM((2, 2, 2, hidden, lon), F32),
+            pltpu.VMEM((2, 2, hidden, lon), F32),
+            pltpu.VMEM((2, 2, hidden, lon), F32),
             pltpu.VMEM((2, 2, hidden, lon), F32),
             pltpu.VMEM((2, hidden, lon), F32),
-            pltpu.VMEM((2, 2, hidden, lon), F32),
+            pltpu.VMEM((2, 2, 2, hidden, lon), F32),
             pltpu.VMEM((2, 8, lon), F32),
             pltpu.VMEM((4 * lon, lon), BF16),
             pltpu.VMEM((2, 2 * lon, 2 * lon), BF16),
             pltpu.VMEM((2, half, lon), F32),
             pltpu.VMEM((peers, half, lon), F32),
-            pltpu.VMEM((half, lon), F32),
+            pltpu.VMEM((peers, half, lon), F32),
             pltpu.VMEM((STEPS + 1, 2, 2, cpad, lon), BF16),
             pltpu.VMEM((STEPS, 2, 2, cpad, lon), BF16),
             pltpu.VMEM((STEPS, 2, half, lon), F32),
@@ -733,8 +819,7 @@
             dma((10,)),
             dma((4,)),
             dma((4,)),
-            dma((2, STEPS, 2)),
-            dma((2, 2, 2)),
+            dma((2, STEPS, 2, 2)),
             dma((2, STEPS)),
             dma((2, STEPS)),
             dma((STEPS, peers, 2)),

time: 21.4 us -> 19.9 us (0.930)
  Pallas kernels: 19.9 us -> 18.5 us
    pallas_call x1, Pallas kernels: 19.1 us -> 17.7 us  [body(): pl.pallas_call(functools.partial(kernel, rows, lon, n_hor, n_lat), out_sh...]
where the time goes in v3:
time: 19.9 us; the launch traced here: 19.8 us
  Pallas kernels  18.5 us (93%)
  between operations  1.29 us (6%)
    pallas_call x1, Pallas kernels, body(): pl.pallas_call(functools.partial(kernel, rows, lon, n_hor, n_lat), out_sh...  17.7 us
    pallas_call x1, Pallas kernels, body(): pl.pallas_call(write, out_shape=(flat, flat), in_specs=[vmem, vmem], out_...  0.82 us

profile of v3, /device:TPU:1, one launch (start us, length us, event | category | flops | bytes accessed | tf_op | source)
XLA Modules:
  0.0 19.8 jit_solution(3426059586526898116)
XLA Ops:
  1.3 17.7 %shard_map.113 = (f32[552,128]{1,0:T(8,128)S(1)}, f32[552,128]{1,0:T(8,128)S(1)}) custom-call(s32[1]{0:T(128)S(6)} %copy.12.lvl_h, f32[64]{0:T(128)} %plan_h.1, f32[552,128]{1,0:T(8,128)} %bitcast.7, f32[552,128]{1,0:T(8,128)} %bitcast.8, f32[1,192]{1,0:T(1,128)} %ret_h.1, f32[1,192]{1,0:T(1,128)} %bitcast.10, f32[1,192]{1,0:T(1,128)} %bitcast.11, ...), custom_call_target="tpu_custom_call" | custom-call | tf_op jit(solution)/shard_map/pallas_call | solution.py:769
  19.0 0.8 %shard_map.114 = (f32[552,128]{1,0:T(8,128)}, f32[552,128]{1,0:T(8,128)}) custom-call(f32[552,128]{1,0:T(8,128)S(1)} %get-tuple-element.6.a, f32[552,128]{1,0:T(8,128)S(1)} %get-tuple-element.7.b), custom_call_target="tpu_custom_call" | custom-call | tf_op jit(solution)/shard_map/pallas_call | solution.py:849

commit v4 on v3

--- a/solution.py
+++ b/solution.py
@@ -81,7 +81,6 @@
     rest_recv,
     fin_recv,
     l_sem,
-    c_sem,
     g_sem,
     h_sem,
     f_sem,
@@ -90,8 +89,7 @@
     q_rsem,
     rf_ssem,
     rf_rsem,
-    r_ssem,
-    r_rsem,
+    r_sem,
     e_sem,
 ):
     hidden, chans = liftw.shape
@@ -139,8 +137,8 @@
     for d in range(1, n_hor):
         greet({"hor": lax.rem(hor + d, n_hor)})
 
-    pairs = [(win_h, win), (lvl_h, lvl), (plan_h, plan)]
-    pairs += [(msc_h, msc), (msh_h, msh), (ret_h, rets.at[core]), (lift_h, liftt)]
+    pairs = [(lift_h, liftt), (lvl_h, lvl), (plan_h, plan)]
+    pairs += [(msc_h, msc), (msh_h, msh), (ret_h, rets.at[core]), (win_h, win)]
     pairs += [(convw_h, convw), (outw_h, outw)]
     loads = [pltpu.make_async_copy(a, b, l_sem.at[i]) for i, (a, b) in enumerate(pairs)]
     fresh_load = pltpu.make_async_copy(fresh_h, arr, l_sem.at[len(pairs)])
@@ -204,31 +202,43 @@
     def joint(g, c):
         return 1 - g if c else g
 
-    sig_copy = remote(sig.at[core], sig.at[core], g_sem.at[0], g_sem.at[1], partner)
-    ret_copy = remote(rets.at[core], rets.at[core], g_sem.at[2], g_sem.at[3], partner)
-    cur_copy = remote(csend, cur.at[core], c_sem.at[0], c_sem.at[1], partner)
-    x_copy = remote(xsend, xrecv, c_sem.at[2], c_sem.at[3], partner)
-
-    def halo_copy(s, side, f):
+    sig_copy = remote(sig.at[core], sig.at[core], l_sem.at[2], g_sem.at[0], partner)
+    ret_copy = remote(rets.at[core], rets.at[core], l_sem.at[3], g_sem.at[1], partner)
+    cur_copy = remote(csend, cur.at[core], l_sem.at[4], g_sem.at[2], partner)
+    x_copy = remote(xsend, xrecv, l_sem.at[5], g_sem.at[3], partner)
+
+    def beside(side):
+        return {"hor": 2 * chip + 1, "lat": lat - 1 + 2 * side}
+
+    def first_halo(side, f):
         return remote(
-            hsend.at[s, side, f],
-            hrecv.at[s, 1 - side, f],
-            h_sem.at[0, s, side, f],
-            h_sem.at[1, s, 1 - side, f],
-            {"hor": 2 * chip + 1, "lat": lat - 1 + 2 * side},
+            hsend.at[0, side, f],
+            hrecv.at[0, 1 - side, f],
+            l_sem.at[side],
+            h_sem.at[f, 1 - side],
+            beside(side),
         )
 
+    def halo_copy(s, side):
+        return remote(
+            hsend.at[s, side],
+            hrecv.at[s, 1 - side],
+            l_sem.at[side],
+            h_sem.at[2 * lax.rem(s, 2), 1 - side],
+            beside(side),
+        )
+
     def feat_copy(s):
-        return remote(fsend.at[s], frecv.at[s], f_sem.at[0, s], f_sem.at[1, s], partner)
+        return remote(fsend.at[s], frecv.at[s], l_sem.at[6], f_sem.at[lax.rem(s, 2)], partner)
 
     def pool_copy(s):
-        return remote(psend.at[s], precv.at[s], p_sem.at[0, s], p_sem.at[1, s], partner)
+        return remote(psend.at[s], precv.at[s], p_sem.at[2], p_sem.at[lax.rem(s, 2)], partner)
 
     def far_pool_copy(s, d, to):
         return remote(
             qsend.at[s],
             qrecv.at[s, d - 1, core],
-            q_ssem.at[s, d - 1, to],
+            q_ssem.at[d - 1, to],
             q_rsem.at[s, d - 1, core],
             {"hor": 2 * (chip + d) + to},
         )
@@ -237,7 +247,7 @@
         return remote(
             qsend.at[s],
             qrecv.at[s, d - 1, c],
-            q_ssem.at[s, d - 1, 0],
+            q_ssem.at[d - 1, 0],
             q_rsem.at[s, d - 1, c],
             {"hor": 2 * chip + c},
         )
@@ -254,19 +264,21 @@
     back = {"hor": 2 * chip - 1}
 
     def base_copy(c):
-        return remote(base_send, base_recv.at[c], r_ssem.at[0], r_rsem.at[0, c], back)
-
-    def rest_copy(stage, c):
+        return remote(base_send, base_recv.at[c], l_sem.at[2], r_sem.at[c], back)
+
+    def outer_rest(stage):
         return remote(
             rest_send.at[stage],
-            rest_recv.at[c, stage],
-            r_ssem.at[1 + stage],
-            r_rsem.at[1 + stage, c],
+            rest_recv.at[1, stage],
+            l_sem.at[3 + stage],
+            r_sem.at[2 + stage],
             back,
         )
 
+    inner_rest = remote(rest_send, rest_recv.at[0], l_sem.at[3], r_sem.at[4], back)
+
     def final_copy(f):
-        return remote(cur.at[f], fin_recv.at[f], e_sem.at[0, f], e_sem.at[1, f], partner)
+        return remote(cur.at[f], fin_recv.at[f], l_sem.at[5 + f], e_sem.at[f], partner)
 
     def half_silu(h):
         return h + h * jnp.tanh(h)
@@ -316,7 +328,15 @@
                 def _():
                     far_pool_copy(s, d, to).start()
 
-    for load in loads[0:3]:
+    def drain_far_pool(s):
+        for d in range(1, n_chip):
+            for to in range(2):
+
+                @pl.when(chip + d < n_chip)
+                def _():
+                    far_pool_copy(s, d, to).wait_send()
+
+    for load in loads[0:6]:
         load.wait()
     sub = lax.broadcasted_iota(jnp.int32, (sig.shape[1], lon), 0)
     levels = jnp.ones((sig.shape[1], lon), F32)
@@ -324,6 +344,17 @@
         levels = jnp.where(sub == s, plan[jnp.maximum(lvl[0] - s, 0)], levels)
     sig[core] = levels
     scale = in_scale_of(levels[0:1, :])
+    mods[0] = jnp.broadcast_to(column(msc[...], 0, hidden), (hidden, lon))
+    mods[1] = jnp.broadcast_to(column(msh[...], 0, hidden), (hidden, lon))
+    eye = (
+        lax.broadcasted_iota(jnp.int32, (chans, chans), 0)
+        == lax.broadcasted_iota(jnp.int32, (chans, chans), 1)
+    ).astype(F32).astype(BF16)
+    liftw[...] = lax.dot_general(
+        liftt[...], eye, (((0,), (0,)), ((), ())), preferred_element_type=F32
+    ).astype(BF16)
+    set_modulation(0, core)
+    loads[6].wait()
     for side, row in enumerate((0, rows - 1)):
         edge_row = win[pl.ds(row, chans, stride=rows), :]
         hsend[0, side, core, 0:chans, :] = (edge_row * scale).astype(BF16)
@@ -336,18 +367,6 @@
             xsend[2 * g + r] = (csend[g, r] * scale).astype(BF16)
         joint_row = jnp.where(outer, 1 + g * (rows - 3), 2 + g * (rows - 5))
         xsend[4 + g] = (home[joint_row] * scale).astype(BF16)
-    for load in loads[3:7]:
-        load.wait()
-    mods[0] = jnp.broadcast_to(column(msc[...], 0, hidden), (hidden, lon))
-    mods[1] = jnp.broadcast_to(column(msh[...], 0, hidden), (hidden, lon))
-    eye = (
-        lax.broadcasted_iota(jnp.int32, (chans, chans), 0)
-        == lax.broadcasted_iota(jnp.int32, (chans, chans), 1)
-    ).astype(F32).astype(BF16)
-    liftw[...] = lax.dot_general(
-        liftt[...], eye, (((0,), (0,)), ((), ())), preferred_element_type=F32
-    ).astype(BF16)
-    set_modulation(0, core)
     for p in range(rows // 2):
         scaled = jnp.concatenate(
             [(home[2 * p + i] * scale).astype(BF16) for i in range(2)], axis=1
@@ -362,7 +381,7 @@
 
         @pl.when(has(side) & when)
         def _():
-            halo_copy(0, side, core).start()
+            first_halo(side, core).start()
 
     sig_copy.start()
     x_copy.start()
@@ -400,7 +419,7 @@
                     place(feats0[row_of(g, r)].astype(F32), c, g, r)
                 frecv[0, g, c] = feats0[(2 + g * (rows - 5)) if c else (1 + g * (rows - 3))]
             convolve(c, c, 0)
-            remote(sig.at[1 - c], sig.at[1 - c], g_sem.at[0], g_sem.at[1], partner).wait_recv()
+            remote(sig.at[1 - c], sig.at[1 - c], l_sem.at[2], g_sem.at[0], partner).wait_recv()
             set_modulation(0, 1 - c)
             x_copy.wait_recv()
             for p in range(3):
@@ -414,9 +433,17 @@
                         frecv[0, i, 1 - c] = feat.astype(BF16)
             convolve(1 - c, c, 0)
 
-    remote(rets.at[other], rets.at[other], g_sem.at[2], g_sem.at[3], partner).wait_recv()
+    remote(rets.at[other], rets.at[other], l_sem.at[3], g_sem.at[1], partner).wait_recv()
     rate[other] = packed_rate(rets[other])
-    remote(csend, cur.at[other], c_sem.at[0], c_sem.at[1], partner).wait_recv()
+    remote(csend, cur.at[other], l_sem.at[4], g_sem.at[2], partner).wait_recv()
+    for copy in (sig_copy, ret_copy, cur_copy, x_copy):
+        copy.wait_send()
+    for side in range(2):
+
+        @pl.when(has(side))
+        def _():
+            first_halo(side, core).wait_send()
+
     def far_rates():
         for d in range(1, n_chip):
 
@@ -463,12 +490,18 @@
                 for f in range(2):
                     acc[f][g, j] += extra[:, f * lon : (f + 1) * lon]
 
-        def await_halos(f):
+        def await_halos():
             for side in range(2):
-
-                @pl.when(has(side))
+                if not final:
+
+                    @pl.when(has(side) & (s == 0))
+                    def _():
+                        for f in range(2):
+                            first_halo(1 - side, f).wait_recv()
+
+                @pl.when(has(side) & (s > 0))
                 def _():
-                    halo_copy(s, 1 - side, f).wait_recv()
+                    halo_copy(s, 1 - side).wait_recv()
 
         def remote_edges(frames):
             near = [hrecv[s, side, f, 0:chans, :] for side in range(2) for f in frames]
@@ -540,10 +573,10 @@
                         nxt - base_send[g, r, 0:chans, :].astype(F32)
                     ).astype(BF16)
 
-        def send_rest(stage):
+        def send_rest(copy):
             @pl.when(chip > 0)
             def _():
-                rest_copy(stage, core).start()
+                copy.start()
 
         def lift(pairs):
             for pair in pairs:
@@ -556,22 +589,28 @@
                     place(modulate(lifted[:, i * lon : (i + 1) * lon], s + 1, f), *cell)
 
         def send_feats(c):
+            @pl.when(s > 0)
+            def _():
+                feat_copy(s).wait_send()
+
             for f in range(2):
                 for g in range(2):
                     fsend[s + 1, g, f] = feature(f, g, joint(g, c))
             feat_copy(s + 1).start()
 
         def send_pools():
-            flat = [
-                jnp.concatenate([feature(f, g, r) for g in range(2) for r in range(2)], axis=1)
-                for f in range(2)
-            ]
-            pooled = dot(jnp.concatenate(flat, axis=0), poolm[...])
+            pooled = None
+            for cells in (near_cells, edge_cells):
+                flat = [jnp.concatenate([feature(*cell) for cell in cells[f]], axis=1) for f in range(2)]
+                part = dot(jnp.concatenate(flat, axis=0), poolm[lon : 3 * lon, :])
+                pooled = part if pooled is None else pooled + part
             first, second = (packed(pooled[f * hidden : (f + 1) * hidden]) for f in range(2))
             qsend[s + 1] = (rate[1] * first + second).astype(WIRE)
+            drain_far_pool(s)
             send_far_pool(s + 1)
             psend[s + 1, 0] = first
             psend[s + 1, 1] = second
+            pool_copy(s).wait_send()
             pool_copy(s + 1).start()
 
         near_cells = [[(f, 0, 1), (f, 1, 0)] for f in range(2)]
@@ -580,12 +619,21 @@
         def send_edges():
             for side, when in send_order:
 
+                @pl.when(has(side) & when & (s > 0))
+                def _():
+                    halo_copy(s, side).wait_send()
+
                 @pl.when(has(side) & when)
                 def _():
-                    for f in range(2):
-                        halo_copy(s + 1, side, f).start()
+                    halo_copy(s + 1, side).start()
 
         all_near, all_edge = near_cells[0] + near_cells[1], edge_cells[0] + edge_cells[1]
+
+        def lift_near():
+            for f in range(2):
+                set_modulation(s + 1, f)
+            lift(near_cells)
+            send_feats(1)
 
         @pl.when(outer)
         def _():
@@ -593,13 +641,20 @@
             contexts()
             finish(all_near)
             if final:
-                send_rest(0)
-            for f in range(2):
-                await_halos(f)
+                send_rest(outer_rest(0))
+
+            if not final:
+
+                @pl.when(chip == 0)
+                def _():
+                    lift_near()
+
+            await_halos()
             remote_edges([0, 1])
             finish(all_edge)
             if final:
-                send_rest(1)
+                send_rest(outer_rest(1))
+                feat_copy(s).wait_send()
             else:
                 send_edges()
 
@@ -607,10 +662,11 @@
                 for f in range(2):
                     final_copy(f).start()
             else:
-                for f in range(2):
-                    set_modulation(s + 1, f)
-                lift(near_cells)
-                send_feats(1)
+
+                @pl.when(chip > 0)
+                def _():
+                    lift_near()
+
                 lift(edge_cells)
                 send_pools()
                 feat_copy(s + 1).wait_recv()
@@ -625,8 +681,8 @@
             contexts()
             if final:
                 finish(near_cells[0] + edge_cells[0])
-                send_rest(0)
-                send_rest(1)
+                send_rest(inner_rest)
+                feat_copy(s).wait_send()
                 finish(near_cells[1] + edge_cells[1])
                 final_copy(1).start()
             else:
@@ -670,14 +726,15 @@
         def _():
             for c in range(2):
                 base_copy(c).wait_recv()
-            for stage in range(2):
-                for c in range(2):
-                    rest_copy(stage, c).wait_recv()
-                    for g in range(2):
-                        r = g if stage else 1 - g
-                        row = outer_row(g, r) if c else inner_row(g, r)
-                        value = base_recv[c, g, r, 0:chans, :].astype(F32)
-                        put(arr, row, value + rest_recv[c, stage, g, 0:chans, :].astype(F32))
+            inner_rest.wait_recv()
+            for c, stage in ((0, 0), (0, 1), (1, 0), (1, 1)):
+                if c:
+                    outer_rest(stage).wait_recv()
+                for g in range(2):
+                    r = g if stage else 1 - g
+                    row = outer_row(g, r) if c else inner_row(g, r)
+                    value = base_recv[c, g, r, 0:chans, :].astype(F32)
+                    put(arr, row, value + rest_recv[c, stage, g, 0:chans, :].astype(F32))
 
     @pl.when(jnp.logical_not(outer))
     def _():
@@ -689,22 +746,9 @@
             for g, r in cells:
                 put(out, outer_row(g, r), fin_recv[f, g, r])
 
-    for copy in (sig_copy, ret_copy, cur_copy, x_copy, final_copy(1)):
-        copy.wait_send()
-    for side in range(2):
-
-        @pl.when(has(side))
-        def _():
-            halo_copy(0, side, core).wait_send()
-
-    for d in range(1, n_chip):
-        for to in range(2):
-
-            @pl.when(chip + d < n_chip)
-            def _():
-                for s in range(STEPS):
-                    far_pool_copy(s, d, to).wait_send()
-
+    final_copy(1).wait_send()
+    pool_copy(STEPS - 1).wait_send()
+    drain_far_pool(STEPS - 1)
     for d in range(1, n_chip):
         for to in range(2):
 
@@ -712,16 +756,11 @@
             def _():
                 far_rate_copy(d, to, core).wait_send()
 
-    for s in range(STEPS):
-        pool_copy(s).wait_send()
-        if s:
-            feat_copy(s).wait_send()
-            for side in range(2):
-
-                @pl.when(outer & has(side))
-                def _():
-                    for f in range(2):
-                        halo_copy(s, side, f).wait_send()
+    for side in range(2):
+
+        @pl.when(outer & has(side))
+        def _():
+            halo_copy(STEPS - 1, side).wait_send()
 
     @pl.when(outer)
     def _():
@@ -730,8 +769,15 @@
     @pl.when(chip > 0)
     def _():
         base_copy(core).wait_send()
+
+    @pl.when((chip > 0) & outer)
+    def _():
         for stage in range(2):
-            rest_copy(stage, core).wait_send()
+            outer_rest(stage).wait_send()
+
+    @pl.when((chip > 0) & jnp.logical_not(outer))
+    def _():
+        inner_rest.wait_send()
 
 
 def write(a, b, a_out, b_out, sem):
@@ -818,17 +864,15 @@
             pltpu.VMEM((2, 2, 2, chans, lon), F32),
             dma((10,)),
             dma((4,)),
-            dma((4,)),
-            dma((2, STEPS, 2, 2)),
-            dma((2, STEPS)),
-            dma((2, STEPS)),
-            dma((STEPS, peers, 2)),
+            dma((3, 2)),
+            dma((2,)),
+            dma((3,)),
+            dma((peers, 2)),
             dma((STEPS, peers, 2)),
             dma((peers, 2)),
             dma((peers, 2)),
-            dma((3,)),
-            dma((3, 2)),
-            dma((2, 2)),
+            dma((5,)),
+            dma((2,)),
         ],
         compiler_params=pltpu.CompilerParams(
             collective_id=0, has_side_effects=True, vmem_limit_bytes=66400000

time: 19.9 us -> 19.4 us (0.975)
  Pallas kernels: 18.5 us -> 18 us
    pallas_call x1, Pallas kernels: 17.7 us -> 17.2 us  [body(): pl.pallas_call(functools.partial(kernel, rows, lon, n_hor, n_lat), out_sh...]
where the time goes in v4:
time: 19.4 us; the launch traced here: 19.3 us
  Pallas kernels  18 us (93%)
  between operations  1.29 us (7%)
    pallas_call x1, Pallas kernels, body(): pl.pallas_call(functools.partial(kernel, rows, lon, n_hor, n_lat), out_sh...  17.2 us
    pallas_call x1, Pallas kernels, body(): pl.pallas_call(write, out_shape=(flat, flat), in_specs=[vmem, vmem], out_...  0.82 us

profile of v4, /device:TPU:1, one launch (start us, length us, event | category | flops | bytes accessed | tf_op | source)
XLA Modules:
  0.0 19.3 jit_solution(16175678147406047979)
XLA Ops:
  1.3 17.2 %shard_map.113 = (f32[552,128]{1,0:T(8,128)S(1)}, f32[552,128]{1,0:T(8,128)S(1)}) custom-call(s32[1]{0:T(128)S(6)} %copy.12.lvl_h, f32[64]{0:T(128)} %plan_h.1, f32[552,128]{1,0:T(8,128)} %bitcast.7, f32[552,128]{1,0:T(8,128)} %bitcast.8, f32[1,192]{1,0:T(1,128)} %ret_h.1, f32[1,192]{1,0:T(1,128)} %bitcast.10, f32[1,192]{1,0:T(1,128)} %bitcast.11, ...), custom_call_target="tpu_custom_call" | custom-call | tf_op jit(solution)/shard_map/pallas_call | solution.py:815
  18.5 0.8 %shard_map.114 = (f32[552,128]{1,0:T(8,128)}, f32[552,128]{1,0:T(8,128)}) custom-call(f32[552,128]{1,0:T(8,128)S(1)} %get-tuple-element.6.a, f32[552,128]{1,0:T(8,128)S(1)} %get-tuple-element.7.b), custom_call_target="tpu_custom_call" | custom-call | tf_op jit(solution)/shard_map/pallas_call | solution.py:893

commit v5 on v4

--- a/solution.py
+++ b/solution.py
@@ -232,7 +232,7 @@
         return remote(fsend.at[s], frecv.at[s], l_sem.at[6], f_sem.at[lax.rem(s, 2)], partner)
 
     def pool_copy(s):
-        return remote(psend.at[s], precv.at[s], p_sem.at[2], p_sem.at[lax.rem(s, 2)], partner)
+        return remote(psend.at[s], precv.at[s], l_sem.at[7], p_sem.at[lax.rem(s, 2)], partner)
 
     def far_pool_copy(s, d, to):
         return remote(
@@ -374,6 +374,10 @@
         lifted = dot(liftw[...], scaled)
         for i in range(2):
             feats0[2 * p + i] = modulate(lifted[:, i * lon : (i + 1) * lon], 0, core).astype(BF16)
+    rate[core] = packed_rate(rets[core])
+    for load in loads[7:]:
+        load.wait()
+    taps[...] = jnp.concatenate([convw[a] for a in range(3)], axis=1)
     pl.semaphore_wait(barrier, n_hor - 1 + n_near * (1 + core))
     even = lax.rem(lat, 2) == 0
     send_order = [(0, even), (1, lat >= 0), (0, jnp.logical_not(even))]
@@ -397,7 +401,6 @@
     psend[0, other] = jnp.zeros((half, lon), F32)
     send_far_pool(0)
     pool_copy(0).start()
-    rate[core] = packed_rate(rets[core])
     for d in range(1, n_chip):
         for to in range(2):
 
@@ -405,9 +408,6 @@
             def _():
                 far_rate_copy(d, to, core).start()
 
-    for load in loads[7:]:
-        load.wait()
-    taps[...] = jnp.concatenate([convw[a] for a in range(3)], axis=1)
 
     for c in range(2):
 
@@ -504,15 +504,16 @@
                     halo_copy(s, 1 - side).wait_recv()
 
         def remote_edges(frames):
-            near = [hrecv[s, side, f, 0:chans, :] for side in range(2) for f in frames]
-            near = dot(liftw[...], jnp.concatenate(near, axis=1))
+            sides = []
             for side in range(2):
-                rhs = []
+                near = [hrecv[s, side, f, 0:chans, :] for f in frames]
+                near = dot(liftw[...], jnp.concatenate(near, axis=1))
+                sides.append([])
                 for i, f in enumerate(frames):
-                    at = (side * len(frames) + i) * lon
-                    feat = modulate(near[:, at : at + lon], s, f)
-                    rhs.append(shifted(jnp.where(has(side), feat, 0.0)))
-                extra = dot(convw[2 * side], jnp.concatenate(rhs, axis=1))
+                    feat = modulate(near[:, i * lon : (i + 1) * lon], s, f)
+                    sides[side].append(shifted(jnp.where(has(side), feat, 0.0)))
+            for side in range(2):
+                extra = dot(convw[2 * side], jnp.concatenate(sides[side], axis=1))
                 for i, f in enumerate(frames):
                     acc[f][side, side] += extra[:, i * lon : (i + 1) * lon]
 
@@ -866,7 +867,7 @@
             dma((4,)),
             dma((3, 2)),
             dma((2,)),
-            dma((3,)),
+            dma((2,)),
             dma((peers, 2)),
             dma((STEPS, peers, 2)),
             dma((peers, 2)),

time: 19.4 us -> 19.4 us (level)
  no operation moved by 1% of the time
where the time goes in v5:
time: 19.4 us; the launch traced here: 19.3 us
  Pallas kernels  18 us (93%)
  between operations  1.29 us (7%)
    pallas_call x1, Pallas kernels, body(): pl.pallas_call(functools.partial(kernel, rows, lon, n_hor, n_lat), out_sh...  17.2 us
    pallas_call x1, Pallas kernels, body(): pl.pallas_call(write, out_shape=(flat, flat), in_specs=[vmem, vmem], out_...  0.82 us

profile of v5, /device:TPU:1, one launch (start us, length us, event | category | flops | bytes accessed | tf_op | source)
XLA Modules:
  0.0 19.3 jit_solution(17536953375200681467)
XLA Ops:
  1.3 17.2 %shard_map.113 = (f32[552,128]{1,0:T(8,128)S(1)}, f32[552,128]{1,0:T(8,128)S(1)}) custom-call(s32[1]{0:T(128)S(6)} %copy.12.lvl_h, f32[64]{0:T(128)} %plan_h.1, f32[552,128]{1,0:T(8,128)} %bitcast.7, f32[552,128]{1,0:T(8,128)} %bitcast.8, f32[1,192]{1,0:T(1,128)} %ret_h.1, f32[1,192]{1,0:T(1,128)} %bitcast.10, f32[1,192]{1,0:T(1,128)} %bitcast.11, ...), custom_call_target="tpu_custom_call" | custom-call | tf_op jit(solution)/shard_map/pallas_call | solution.py:816
  18.4 0.8 %shard_map.114 = (f32[552,128]{1,0:T(8,128)}, f32[552,128]{1,0:T(8,128)}) custom-call(f32[552,128]{1,0:T(8,128)S(1)} %get-tuple-element.6.a, f32[552,128]{1,0:T(8,128)S(1)} %get-tuple-element.7.b), custom_call_target="tpu_custom_call" | custom-call | tf_op jit(solution)/shard_map/pallas_call | solution.py:894

commit v6 on v4

--- a/solution.py
+++ b/solution.py
@@ -697,8 +697,7 @@
                 for f in range(2):
                     convolve(f, 0, s + 1)
 
-    @pl.loop(0, STEPS - 1)
-    def _(s):
+    for s in range(STEPS - 1):
         step(s, False)
 
     step(STEPS - 1, True)

time: 19.4 us -> 19.5 us (level)
  no operation moved by 1% of the time
where the time goes in v6:
time: 19.5 us; the launch traced here: 19.4 us
  Pallas kernels  17.9 us (92%)
  between operations  1.45 us (7%)
    pallas_call x1, Pallas kernels, body(): pl.pallas_call(functools.partial(kernel, rows, lon, n_hor, n_lat), out_sh...  17.1 us
    pallas_call x1, Pallas kernels, body(): pl.pallas_call(write, out_shape=(flat, flat), in_specs=[vmem, vmem], out_...  0.82 us

profile of v6, /device:TPU:1, one launch (start us, length us, event | category | flops | bytes accessed | tf_op | source)
XLA Modules:
  0.0 19.4 jit_solution(9646728009866764114)
XLA Ops:
  1.3 17.1 %shard_map.113 = (f32[552,128]{1,0:T(8,128)S(1)}, f32[552,128]{1,0:T(8,128)S(1)}) custom-call(s32[1]{0:T(128)S(6)} %copy.12.lvl_h, f32[64]{0:T(128)} %plan_h.1, f32[552,128]{1,0:T(8,128)} %bitcast.7, f32[552,128]{1,0:T(8,128)} %bitcast.8, f32[1,192]{1,0:T(1,128)} %ret_h.1, f32[1,192]{1,0:T(1,128)} %bitcast.10, f32[1,192]{1,0:T(1,128)} %bitcast.11, ...), custom_call_target="tpu_custom_call" | custom-call | tf_op jit(solution)/shard_map/pallas_call | solution.py:814
  18.4 0.8 %shard_map.114 = (f32[552,128]{1,0:T(8,128)}, f32[552,128]{1,0:T(8,128)}) custom-call(f32[552,128]{1,0:T(8,128)S(1)} %get-tuple-element.6.a, f32[552,128]{1,0:T(8,128)S(1)} %get-tuple-element.7.b), custom_call_target="tpu_custom_call" | custom-call | tf_op jit(solution)/shard_map/pallas_call | solution.py:892
